TPU v7x, 256 devices: a whole 4x4x8 slice. The times are simulated.
256 devices in a mesh: dp: 8 (over y, x_hi), head: 32 (over z, x_lo, core).
Axes of the slice: x: 4 (x_hi: 2, x_lo: 2; x = x_hi * 2 + x_lo), y: 4, z: 8, core: 2. Of those that a mesh axis runs over, the one named last changes fastest.
Arguments:
- query_latent: bfloat16 [2048, 1536], P('dp'), may hold values from -384 to 384
- kv_latent: bfloat16 [2048, 576], P('dp'), may hold values from -48 to 48
- out_grad: bfloat16 [2048, 16384], P('dp', 'head'), may hold values from -20 to 20
- query_up: bfloat16 [1536, 24576], P(None, 'head'), may hold values from -1 to 1
- key_up: bfloat16 [512, 16384], P(None, 'head'), may hold values from -0.25 to 0.25
- value_up: bfloat16 [512, 16384], P(None, 'head'), may hold values from -0.25 to 0.25
Outputs:
- query_latent_grad: float32 [2048, 1536], P(('dp', 'head'))
- kv_latent_grad: float32 [2048, 576], P(('dp', 'head'))
- query_up_grad: bfloat16 [1536, 24576], P(None, 'head')
- key_up_grad: bfloat16 [512, 16384], P(None, 'head')
- value_up_grad: bfloat16 [512, 16384], P(None, 'head')
All inputs are finite; a program needn't handle non-finite values.
Results may differ from a plain program's by a relative error of at most 0.035.
Values may be sent and summed in bfloat16 or wider, within the bound.
A program may use at most 64 MiB of HBM per device.

v0:
```python
import jax
import jax.numpy as jnp
from jax import lax
from jax.sharding import PartitionSpec as P

QL = 1536
KL = 512
DN = 128
DR = 64


max_rms = 1.0
eps = 1e-06


def rotate(values, length):
    half = values.shape[-1] // 2
    freqs = 10000.0 ** (-2.0 * jnp.arange(half, dtype=jnp.float32) / values.shape[-1])
    angle = jnp.arange(length, dtype=jnp.float32)[:, None] * freqs[None, :]
    cosine = jnp.cos(angle)[:, None, :]
    sine = jnp.sin(angle)[:, None, :]
    first = values[..., :half]
    second = values[..., half:]
    return jnp.concatenate(
        [first * cosine - second * sine, second * cosine + first * sine], axis=-1
    )


def attend(q_plain, q_rot, keys, key_rot, values):
    length = q_plain.shape[0]
    q_rope = rotate(q_rot.astype(jnp.float32), length).astype(jnp.bfloat16)
    scale = 1.0 / (q_plain.shape[-1] + q_rot.shape[-1]) ** 0.5
    scores = jnp.einsum("shd,thd->hst", q_plain, keys, preferred_element_type=jnp.float32)
    scores = scores + jnp.einsum(
        "shd,thd->hst", q_rope, key_rot, preferred_element_type=jnp.float32
    )
    scores = scores * scale
    positions = jnp.arange(length)
    allowed = positions[None, :] <= positions[:, None]
    scores = jnp.where(allowed[None], scores, -jnp.inf)
    top = lax.stop_gradient(jnp.max(scores, axis=-1, keepdims=True))
    weights = jnp.exp(scores - top)
    probs = (weights / jnp.sum(weights, axis=-1, keepdims=True)).astype(jnp.bfloat16)
    return jnp.einsum("hst,thd->shd", probs, values, preferred_element_type=jnp.float32)


def transposed(left, right):
    return lax.dot_general(
        left, right, (((1,), (1,)), ((), ())), preferred_element_type=jnp.float32
    )


def squares(grads):
    return (
        jnp.sum(grads[0] * grads[0]) + jnp.sum(grads[1] * grads[1]) + jnp.sum(grads[2] * grads[2])
    )


def per_device(query_latent, kv_latent, out_grad, query_up, key_up, value_up):
    length = query_latent.shape[0]
    heads = key_up.shape[1] // DN
    queries = jnp.dot(query_latent, query_up, preferred_element_type=jnp.float32).astype(
        jnp.bfloat16
    )
    queries = queries.reshape(length, heads, DN + DR)
    plain_latent = kv_latent[:, :KL]
    keys = (
        jnp.dot(plain_latent, key_up, preferred_element_type=jnp.float32)
        .astype(jnp.bfloat16)
        .reshape(length, heads, DN)
    )
    values = (
        jnp.dot(plain_latent, value_up, preferred_element_type=jnp.float32)
        .astype(jnp.bfloat16)
        .reshape(length, heads, DN)
    )
    key_rot = jnp.broadcast_to(kv_latent[:, None, KL:], (length, heads, DR))
    attn, pull = jax.vjp(attend, queries[..., :DN], queries[..., DN:], keys, key_rot, values)
    grad_plain, grad_rot, key_grad, rot_grad, value_grad = pull(
        out_grad.reshape(length, heads, DN).astype(jnp.float32)
    )
    q_grad = jnp.concatenate([grad_plain, grad_rot], axis=-1).reshape(length, heads * (DN + DR))
    key_grad = key_grad.reshape(length, heads * DN)
    value_grad = value_grad.reshape(length, heads * DN)
    rot_sum = jnp.sum(rot_grad.astype(jnp.float32), axis=1)
    term_q = transposed(q_grad, query_up)
    term_kv = transposed(key_grad, key_up) + transposed(value_grad, value_up)
    latent_rows = lax.psum_scatter(
        jnp.concatenate([term_q, term_kv, rot_sum], axis=1), "head", scatter_dimension=0, tiled=True
    )
    query_latent_grad = latent_rows[:, :QL]
    kv_latent_grad = latent_rows[:, QL:]
    grad_wq = jnp.dot(query_latent.T, q_grad, preferred_element_type=jnp.float32)
    grad_wk = jnp.dot(plain_latent.T, key_grad, preferred_element_type=jnp.float32)
    grad_wv = jnp.dot(plain_latent.T, value_grad, preferred_element_type=jnp.float32)
    count = (QL * grad_wq.shape[1] + KL * grad_wk.shape[1] + KL * grad_wv.shape[1]) * lax.axis_size(
        "head"
    )
    limit = max_rms * count**0.5
    summed = lax.psum((grad_wq, grad_wk, grad_wv), "dp")
    total = lax.psum(squares(summed), "head")
    factor = jnp.minimum(1.0, limit / jnp.sqrt(total + eps))
    out_q = (summed[0] * factor).astype(jnp.bfloat16)
    out_k = (summed[1] * factor).astype(jnp.bfloat16)
    out_v = (summed[2] * factor).astype(jnp.bfloat16)
    return (query_latent_grad, kv_latent_grad, out_q, out_k, out_v)


def solution(mesh):
    placed = (
        P("dp", None),
        P("dp", None),
        P("dp", "head"),
        P(None, "head"),
        P(None, "head"),
        P(None, "head"),
    )
    return jax.shard_map(
        per_device,
        mesh=mesh,
        in_specs=placed,
        out_specs=(
            P(("dp", "head"), None),
            P(("dp", "head"), None),
            P(None, "head"),
            P(None, "head"),
            P(None, "head"),
        ),
        check_vma=False,
    )
```

profile of v0, /device:TPU:2, one launch (start us, length us, event | category | flops | bytes accessed | tf_op | source)
XLA Modules:
  0.0 639.1 jit_solution(8632470227194152105)
XLA Ops:
  7.2 0.0 copy-start
  7.2 0.0 copy-start.8
  7.2 0.0 all-reduce.7.cloned.1.call-start
  7.3 0.9 slice.29
  8.2 0.8 fusion.31
  9.0 1.8 copy.63
  10.8 1.4 convolution_convert_fusion.5
  12.3 0.1 copy.65
  12.4 0.0 copy-done.8
  12.4 0.0 copy-start.6
  12.4 2.2 fusion.5
  14.6 1.9 convolution_convert_fusion.1
  16.5 0.2 copy.43
  16.7 0.0 copy-start.4
  16.7 0.3 fusion.21
  17.1 0.8 subtract_convert_fusion
  17.9 0.0 copy-start.14
  17.9 0.0 copy-start.16
  17.9 0.6 copy-done.14
  18.5 0.0 copy-done.16
  18.5 0.4 fusion.4
  18.9 0.0 copy-start.3
  18.9 1.0 copy-done.3
  19.8 0.7 fusion.35
  20.6 2.7 convolution_convert_fusion.2
  23.3 1.4 fusion.18
  24.7 0.2 fusion.15
  25.0 0.0 copy-start.13
  25.0 0.3 convolution_convert_fusion.3
  25.4 0.3 fusion.10
  25.6 0.0 copy-done.7
  25.7 0.2 fusion.6
  25.9 0.2 fusion.9
  26.2 0.1 copy.53
  26.3 1.4 fusion.37
  27.8 0.0 copy-start.12
  27.8 0.8 fusion.36
  28.6 0.1 copy-done.10
  28.7 0.2 copy-done.12
  28.9 0.3 convolution_add_fusion.1
  29.2 0.0 copy-start.9
  29.2 1.5 pad_maximum_fusion
  30.8 0.0 all-reduce.7.cloned.1.call-update
  30.8 0.0 all-reduce.9.cloned.1.call-start
  30.8 0.0 copy-start.11
  30.8 2.3 convolution_bitcast_fusion.1
  33.2 1.3 convolution_bitcast_fusion.2
  34.5 2.9 convolution_bitcast_fusion
  37.5 0.0 all-reduce.9.cloned.1.call-update
  37.5 0.6 copy-done.18
  38.1 0.6 dynamic-slice
  39.4 222.5 %all-reduce.7.cloned.1.call-done = f32[256,2112]{1,0:T(8,128)} async-done(((f32[256,2112]{1,0:T(8,128)}), f32[256,2112]{1,0:T(8,128)}) %all-reduce.7.cloned.1.call-update) | async-done | bytes 2162704
  261.9 1.4 constant_dynamic-slice_fusion
  263.3 292.6 %all-reduce.9.cloned.1.call-done = (f32[1536,768]{0,1:T(8,128)}, f32[512,512]{0,1:T(8,128)}, f32[512,512]{0,1:T(8,128)}) async-done(((f32[1536,768]{0,1:T(8,128)}, f32[512,512]{0,1:T(8,128)}, f32[512,512]{0,1:T(8,128)}), (f32[1536,768]{0,1:T(8,128)}, f32[512,512]{0,1:T(8,128)}, f32[512,512]{0,1:T(8,128)})) %all-reduce.9.cloned.1.call-update) | async-done | bytes 6815760 | tf_op jit(solution)/shard_map/psum | solution.py:100
  555.9 2.1 multiply_reduce_fusion.1
  558.0 2.1 multiply_reduce_fusion.2
  560.1 4.2 multiply_reduce_fusion
  566.2 1.4 dynamic-slice.3
  567.6 52.9 %psum.31 = f32[]{:T(128)} all-reduce(f32[]{:T(128)S(6)} %add.36), channel_id=1, replica_groups=mesh['dp'=8,'head'=32] {'head'}, use_global_device_ids=true, to_apply=%region_11.12 | all-reduce | flops 1 | bytes 8 | tf_op jit(solution)/shard_map/psum | solution.py:101
  621.2 4.5 multiply_convert_fusion
  625.7 0.3 multiply_convert_fusion.1
  626.0 1.0 copy.56
  627.0 4.3 copy.54
  631.3 1.0 copy.55
  (27 shorter events, 0.2 us)
Async XLA Ops:
  7.2 7.4 %copy-start = (bf16[1536,768]{1,0:T(8,128)(2,1)S(1)}, bf16[1536,768]{1,0:T(8,128)(2,1)}, u32[]{:S(2)}) copy-start(bf16[1536,768]{1,0:T(8,128)(2,1)} %param.9) | copy-start | bytes 7077892
  7.2 5.2 copy-start.8
  7.2 254.7 %all-reduce.7.cloned.1.call-start = ((), (), s32[]{:S(2)}) async-start(), calls=%async_computation | async-start | bytes 4456448
  12.4 4.3 copy-start.6
  16.7 1.2 copy-start.4
  17.9 0.6 copy-start.14
  17.9 0.6 copy-start.16
  18.9 1.0 copy-start.3
  23.3 1.7 copy-start.5
  23.3 2.0 copy-start.15
  23.3 2.0 copy-start.17
  24.7 1.0 copy-start.7
  25.0 1.1 copy-start.13
  27.7 1.0 copy-start.10
  27.8 1.1 copy-start.12
  29.2 1.6 copy-start.9
  30.8 525.1 %all-reduce.9.cloned.1.call-start = ((), (), s32[]{:S(2)}) async-start(), calls=%async_computation.1 | async-start | bytes 13631488 | tf_op jit(solution)/shard_map/psum | solution.py:100
  30.8 3.7 copy-start.11
  37.5 0.7 copy-start.18
  621.2 4.5 copy-start.1
  621.2 4.5 copy-start.2
Sparse Core Ops, SparseCore 0:
  30.9 230.9 all-reduce.6
  264.7 291.1 all-reduce.8
where the time goes:
time: 644 us; the launch traced here: 639 us
  waiting for transfers between devices  515 us (80%)
  blocking collectives  52.9 us (8%)
  matrix products  20.5 us (3%)
  between operations  17.7 us (3%)
  other arithmetic  17.3 us (3%)
  local copies, waits for them, and re-layouts  15.4 us (2%)
    psum x1, waiting for transfers between devices, per_device(): summed = lax.psum((grad_wq, grad_wk, grad_wv), 'dp')  293 us
    unnamed x3, waiting for transfers between devices  223 us
    psum x1, blocking collectives, per_device(): total = lax.psum(squares(summed), 'head')  52.9 us
  transfers between devices with their start and end apart: 2, of which 2 were waited for; matrix products, arithmetic and copies ran while one was open for 1% of the time, Pallas kernels for 0%

commit v1 on v0

v1 whole, which is shorter than its diff:
```python
import functools

import jax
import jax.numpy as jnp
from jax import lax
from jax.experimental import pallas as pl
from jax.experimental.pallas import tpu as pltpu
from jax.sharding import PartitionSpec as P

QL = 1536
KL = 512
DN = 128
DR = 64
LAT = 2176

max_rms = 1.0
eps = 1e-06

MESH = pl.DeviceIdType.MESH
BF = jnp.bfloat16
F32 = jnp.float32

PART_ROWS = (768, 768, 512)
PART_COLS = (768, 768, 1024)
ORDERS = ("ABX", "BXA", "XAB")
CHUNK = 32


def rotate(values, length):
    half = values.shape[-1] // 2
    freqs = 10000.0 ** (-2.0 * jnp.arange(half, dtype=jnp.float32) / values.shape[-1])
    angle = jnp.arange(length, dtype=jnp.float32)[:, None] * freqs[None, :]
    cosine = jnp.cos(angle)[:, None, :]
    sine = jnp.sin(angle)[:, None, :]
    first = values[..., :half]
    second = values[..., half:]
    return jnp.concatenate(
        [first * cosine - second * sine, second * cosine + first * sine], axis=-1
    )


def attend(q_plain, q_rot, keys, key_rot, values):
    length = q_plain.shape[0]
    q_rope = rotate(q_rot.astype(jnp.float32), length).astype(jnp.bfloat16)
    scale = 1.0 / (q_plain.shape[-1] + q_rot.shape[-1]) ** 0.5
    scores = jnp.einsum("shd,thd->hst", q_plain, keys, preferred_element_type=jnp.float32)
    scores = scores + jnp.einsum(
        "shd,thd->hst", q_rope, key_rot, preferred_element_type=jnp.float32
    )
    scores = scores * scale
    positions = jnp.arange(length)
    allowed = positions[None, :] <= positions[:, None]
    scores = jnp.where(allowed[None], scores, -jnp.inf)
    top = lax.stop_gradient(jnp.max(scores, axis=-1, keepdims=True))
    weights = jnp.exp(scores - top)
    probs = (weights / jnp.sum(weights, axis=-1, keepdims=True)).astype(jnp.bfloat16)
    return jnp.einsum("hst,thd->shd", probs, values, preferred_element_type=jnp.float32)


def transposed(left, right):
    return lax.dot_general(
        left, right, (((1,), (1,)), ((), ())), preferred_element_type=jnp.float32
    )


def for_rows(rows, step, body):
    def one(i, carry):
        body(pl.multiple_of(i * step, step))
        return carry

    lax.fori_loop(0, rows // step, one, 0)


def places():
    d, h = lax.axis_index("dp"), lax.axis_index("head")
    y, xh = d // 2, d % 2
    b, y0 = y // 2, y % 2
    a = (y0 + b) % 2
    z, r = h // 4, h % 4
    xl, c = r // 2, r % 2
    bits = {"A": a, "B": b, "X": xh}
    peer = {
        "A": (2 * (y + 1 - 2 * y0) + xh, h),
        "B": (2 * (3 - y) + xh, h),
        "X": (2 * y + 1 - xh, h),
        "C": (d, h + 1 - 2 * c),
        "L": (d, h + 2 - 4 * xl),
    }
    for k in range(1, 8):
        peer["Z%d" % k] = (d, (h + 4 * k) % 32)
    return bits, peer, z, xl, c


def greet(peer):
    barrier = pltpu.get_barrier_semaphore()
    for where in peer.values():
        pl.semaphore_signal(barrier, inc=1, device_id=where, device_id_type=MESH)
    pl.semaphore_wait(barrier, len(peer))


def comm_kernel(
    q_ref, kv_ref, lat_ref,
    gq_out, gkv_out, s_out, lat_out,
    stg0, rcv0, redA0, redB0,
    stg1, rcv1, redA1, redB1,
    stg2, rcv2, redA2, redB2,
    gq, gkv,
    lrecv, lsum, zs, zr, lx, lxr,
    sv, sr, sz,
    rs_send, rs_recv, ag_send, ag_recv, l_send, l_recv, s_send, s_recv, out_sem,
):
    bits, peer, z, xl, c = places()
    greet(peer)

    def remote(src, dst, send, recv, where):
        copy = pltpu.make_async_remote_copy(
            src_ref=src, dst_ref=dst, send_sem=send, recv_sem=recv,
            device_id=peer[where], device_id_type=MESH,
        )
        copy.start()
        return copy

    stages = ((stg0, rcv0, redA0, redB0), (stg1, rcv1, redA1, redB1), (stg2, rcv2, redA2, redB2))

    def term(p, lo, n):
        if p == 2:
            return kv_ref[pl.ds(lo, n), :]
        return q_ref[pl.ds(768 * p + lo, n), :]

    def where_rows(p, s):
        rows = PART_ROWS[p]
        return (0, rows // 2, rows // 2 + rows // 4)[s], rows >> (s + 1)

    def source(p, s, lo, n):
        if s == 0:
            return term(p, lo, n)
        return stages[p][1 + s][pl.ds(lo, n), :]

    def rs_start(p, s):
        stg, rcv = stages[p][:2]
        off, n = where_rows(p, s)
        dim = ORDERS[p][s]
        away = (1 - bits[dim]) * n

        def body(i):
            stg[pl.ds(off + i, CHUNK), :] = source(p, s, away + i, CHUNK).astype(BF)

        for_rows(n, CHUNK, body)
        return remote(
            stg.at[pl.ds(off, n)], rcv.at[pl.ds(off, n)],
            rs_send.at[p, s], rs_recv.at[p, s], dim,
        )

    def rs_add(p, s):
        rcv = stages[p][1]
        off, n = where_rows(p, s)
        keep = bits[ORDERS[p][s]] * n
        red = stages[p][2 + s]

        def body(i):
            red[pl.ds(i, CHUNK), :] = source(p, s, keep + i, CHUNK) + rcv[
                pl.ds(off + i, CHUNK), :
            ].astype(F32)

        for_rows(n, CHUNK, body)

    def owned(p, s):
        rows = PART_ROWS[p]
        lo = 0
        for t in range(s + 1):
            lo = lo + bits[ORDERS[p][t]] * (rows >> (t + 1))
        return lo

    def gathered(p, lo, n):
        lo = pl.multiple_of(lo, 32)
        if p == 2:
            return gkv.at[pl.ds(lo, n)]
        return gq.at[pl.ds(768 * p + lo, n)]

    def ag_start(p, s):
        lo, n = owned(p, s), PART_ROWS[p] >> (s + 1)
        block = gathered(p, lo, n)
        return remote(block, block, ag_send.at[p, s], ag_recv.at[p, s], ORDERS[p][s])

    first = [rs_start(p, 0) for p in (2, 0, 1)]
    core = remote(lat_ref.at[:, 1 - c], lrecv, l_send.at[0], l_recv.at[0], "C")
    core.wait()

    def core_body(k, carry):
        lsum[k] = lat_ref[k, c] + lrecv[k]
        return carry

    lax.fori_loop(0, 16, core_body, 0)

    def zs_body(k, carry):
        zs[k] = jnp.concatenate([lsum[2 * k], lsum[2 * k + 1]], axis=0).astype(BF)
        return carry

    lax.fori_loop(0, 8, zs_body, 0)
    zcopies = [
        remote(zs.at[(z + k) % 8], zr.at[k - 1], l_send.at[k], l_recv.at[k], "Z%d" % k)
        for k in range(1, 8)
    ]
    for copy in first:
        copy.wait()
    second = []
    for p in (2, 0, 1):
        rs_add(p, 0)
        second.append(rs_start(p, 1))
    third = []
    for copy, p in zip(second, (2, 0, 1)):
        copy.wait()
        rs_add(p, 1)
        third.append(rs_start(p, 2))
    for copy in zcopies:
        copy.wait()
    lx[0] = lsum[2 * z]
    lx[1] = lsum[2 * z + 1]
    for k in range(7):
        got = zr[k].astype(F32)
        lx[0] = lx[0] + got[:8]
        lx[1] = lx[1] + got[8:]
    xcopy = remote(lx.at[1 - xl], lxr, l_send.at[8], l_recv.at[8], "L")
    sv[0] = jnp.zeros((8, 128), F32)
    for copy, p in zip(third, (2, 0, 1)):
        copy.wait()
        off, n = where_rows(p, 2)
        keep = bits[ORDERS[p][2]] * n
        lo = owned(p, 2)
        rcv, red = stages[p][1], stages[p][3]
        target = gkv if p == 2 else gq
        base = 0 if p == 2 else 768 * p

        def body(i):
            total = red[pl.ds(keep + i, CHUNK), :] + rcv[pl.ds(off + i, CHUNK), :].astype(F32)
            target[pl.ds(pl.multiple_of(base + lo + i, CHUNK), CHUNK), :] = total.astype(BF)
            square = total * total
            part = square[:, :128]
            for j in range(1, PART_COLS[p] // 128):
                part = part + square[:, 128 * j : 128 * (j + 1)]
            sv[0] = sv[0] + part[:8] + part[8:16] + part[16:24] + part[24:32]

        for_rows(n, CHUNK, body)

    def s_step(i, dim):
        return remote(sv.at[i], sr.at[i], s_send.at[i], s_recv.at[i], dim)

    def s_add(copy, i):
        copy.wait()
        sv[i + 1] = sv[i] + sr[i]

    s0 = s_step(0, "A")
    gather = [ag_start(p, 2) for p in (2, 0, 1)]
    s_add(s0, 0)
    s1 = s_step(1, "C")
    xcopy.wait()
    lat_out[...] = lx[xl] + lxr[...]
    s_add(s1, 1)
    s2 = s_step(2, "B")
    later = []
    for copy, p in zip(gather, (2, 0, 1)):
        copy.wait()
        later.append(ag_start(p, 1))
    s_add(s2, 2)
    s3 = s_step(3, "L")
    s_add(s3, 3)
    s4 = s_step(4, "X")
    last = []
    for copy, p in zip(later, (2, 0, 1)):
        copy.wait()
        last.append(ag_start(p, 0))
    s_add(s4, 4)
    szc = [
        remote(sv.at[5], sz.at[z], s_send.at[4 + k], s_recv.at[4 + k], "Z%d" % k)
        for k in range(1, 8)
    ]
    sz[z] = sv[5]
    for copy in szc:
        copy.wait()
    s_out[...] = sz[...]
    outs = []
    for i, (copy, p) in enumerate(zip(last, (2, 0, 1))):
        copy.wait()
        if p == 2:
            out = pltpu.make_async_copy(gkv, gkv_out, out_sem.at[p])
        else:
            out = pltpu.make_async_copy(
                gq.at[pl.ds(768 * p, 768)], gq_out.at[pl.ds(768 * p, 768)], out_sem.at[p]
            )
        out.start()
        outs.append(out)
    for out in outs:
        out.wait()


def communicate(dwq, dwkv, lat):
    scratch = []
    for rows, cols in zip(PART_ROWS, PART_COLS):
        moved = rows // 2 + rows // 4 + rows // 8
        scratch += [
            pltpu.VMEM((moved, cols), BF),
            pltpu.VMEM((moved, cols), BF),
            pltpu.VMEM((rows // 2, cols), F32),
            pltpu.VMEM((rows // 4, cols), F32),
        ]
    scratch += [
        pltpu.VMEM((1536, 768), BF),
        pltpu.VMEM((512, 1024), BF),
        pltpu.VMEM((16, 8, LAT), F32),
        pltpu.VMEM((16, 8, LAT), F32),
        pltpu.VMEM((8, 16, LAT), BF),
        pltpu.VMEM((7, 16, LAT), BF),
        pltpu.VMEM((2, 8, LAT), F32),
        pltpu.VMEM((8, LAT), F32),
        pltpu.VMEM((6, 8, 128), F32),
        pltpu.VMEM((5, 8, 128), F32),
        pltpu.VMEM((8, 8, 128), F32),
        pltpu.SemaphoreType.DMA((3, 3)),
        pltpu.SemaphoreType.DMA((3, 3)),
        pltpu.SemaphoreType.DMA((3, 3)),
        pltpu.SemaphoreType.DMA((3, 3)),
        pltpu.SemaphoreType.DMA((9,)),
        pltpu.SemaphoreType.DMA((9,)),
        pltpu.SemaphoreType.DMA((12,)),
        pltpu.SemaphoreType.DMA((12,)),
        pltpu.SemaphoreType.DMA((3,)),
    ]
    vmem = pl.BlockSpec(memory_space=pltpu.VMEM)
    hbm = pl.BlockSpec(memory_space=pl.ANY)
    return pl.pallas_call(
        comm_kernel,
        out_shape=(
            jax.ShapeDtypeStruct((1536, 768), BF),
            jax.ShapeDtypeStruct((512, 1024), BF),
            jax.ShapeDtypeStruct((8, 8, 128), F32),
            jax.ShapeDtypeStruct((8, LAT), F32),
        ),
        in_specs=[vmem] * 3,
        out_specs=(hbm, hbm, vmem, vmem),
        scratch_shapes=scratch,
        name="comm",
        compiler_params=pltpu.CompilerParams(
            collective_id=0, has_side_effects=True, vmem_limit_bytes=50 << 20
        ),
    )(dwq, dwkv, lat.reshape(16, 2, 8, LAT))


def finish_kernel(count, s_ref, lat_ref, q_ref, kv_ref, ql_out, kvl_out, q_out, k_out, v_out):
    total = jnp.sum(s_ref[...], axis=0)
    total = jnp.sum(total, axis=0, keepdims=True)
    total = jnp.sum(total, axis=1, keepdims=True)
    factor = jnp.minimum(1.0, max_rms * count**0.5 / jnp.sqrt(total + eps))
    q_out[...] = (q_ref[...].astype(F32) * factor).astype(BF)
    k_out[...] = (kv_ref[:, :512].astype(F32) * factor).astype(BF)
    v_out[...] = (kv_ref[:, 512:].astype(F32) * factor).astype(BF)

    @pl.when(pl.program_id(0) == 0)
    def _():
        ql_out[...] = lat_ref[:, :QL]
        kvl_out[...] = lat_ref[:, QL : QL + KL + DR]


def finish(count, s, lat, gq, gkv):
    steps = 4
    return pl.pallas_call(
        functools.partial(finish_kernel, count),
        grid=(steps,),
        out_shape=(
            jax.ShapeDtypeStruct((8, QL), F32),
            jax.ShapeDtypeStruct((8, KL + DR), F32),
            jax.ShapeDtypeStruct((1536, 768), BF),
            jax.ShapeDtypeStruct((512, 512), BF),
            jax.ShapeDtypeStruct((512, 512), BF),
        ),
        in_specs=[
            pl.BlockSpec((8, 8, 128), lambda i: (0, 0, 0)),
            pl.BlockSpec((8, LAT), lambda i: (0, 0)),
            pl.BlockSpec((1536 // steps, 768), lambda i: (i, 0)),
            pl.BlockSpec((512 // steps, 1024), lambda i: (i, 0)),
        ],
        out_specs=(
            pl.BlockSpec((8, QL), lambda i: (0, 0)),
            pl.BlockSpec((8, KL + DR), lambda i: (0, 0)),
            pl.BlockSpec((1536 // steps, 768), lambda i: (i, 0)),
            pl.BlockSpec((512 // steps, 512), lambda i: (i, 0)),
            pl.BlockSpec((512 // steps, 512), lambda i: (i, 0)),
        ),
        name="finish",
    )(s, lat, gq, gkv)


def per_device(query_latent, kv_latent, out_grad, query_up, key_up, value_up):
    length = query_latent.shape[0]
    heads = key_up.shape[1] // DN
    queries = jnp.dot(query_latent, query_up, preferred_element_type=F32).astype(BF)
    queries = queries.reshape(length, heads, DN + DR)
    plain_latent = kv_latent[:, :KL]
    keys = (
        jnp.dot(plain_latent, key_up, preferred_element_type=F32)
        .astype(BF)
        .reshape(length, heads, DN)
    )
    values = (
        jnp.dot(plain_latent, value_up, preferred_element_type=F32)
        .astype(BF)
        .reshape(length, heads, DN)
    )
    key_rot = jnp.broadcast_to(kv_latent[:, None, KL:], (length, heads, DR))
    attn, pull = jax.vjp(attend, queries[..., :DN], queries[..., DN:], keys, key_rot, values)
    grad_plain, grad_rot, key_grad, rot_grad, value_grad = pull(
        out_grad.reshape(length, heads, DN).astype(F32)
    )
    q_grad = jnp.concatenate([grad_plain, grad_rot], axis=-1).reshape(length, heads * (DN + DR))
    key_grad = key_grad.reshape(length, heads * DN)
    value_grad = value_grad.reshape(length, heads * DN)
    rot_sum = jnp.sum(rot_grad.astype(F32), axis=1)
    term_q = transposed(q_grad, query_up)
    term_kv = transposed(key_grad, key_up) + transposed(value_grad, value_up)
    lat = jnp.concatenate(
        [term_q, term_kv, rot_sum, jnp.zeros((length, LAT - QL - KL - DR), F32)], axis=1
    )
    grad_wq = jnp.dot(query_latent.T, q_grad, preferred_element_type=F32)
    grad_wkv = jnp.dot(
        plain_latent.T, jnp.concatenate([key_grad, value_grad], axis=1), preferred_element_type=F32
    )
    width = lax.axis_size("head")
    count = (QL * query_up.shape[1] + 2 * KL * key_up.shape[1]) * width
    gq, gkv, s, lat8 = communicate(grad_wq, grad_wkv, lat)
    return tuple(finish(count, s, lat8, gq, gkv))


def solution(mesh):
    placed = (
        P("dp", None),
        P("dp", None),
        P("dp", "head"),
        P(None, "head"),
        P(None, "head"),
        P(None, "head"),
    )
    return jax.shard_map(
        per_device,
        mesh=mesh,
        in_specs=placed,
        out_specs=(
            P(("dp", "head"), None),
            P(("dp", "head"), None),
            P(None, "head"),
            P(None, "head"),
            P(None, "head"),
        ),
        check_vma=False,
    )
```

time: 644 us -> 117 us (0.18)
  waiting for transfers between devices: 515 us -> 0 us
  Pallas kernels: 0 us -> 75.9 us
  blocking collectives: 52.9 us -> 0 us
  between operations: 17.7 us -> 1 us
  other arithmetic: 17.3 us -> 2.78 us
    psum x1 -> x0, waiting for transfers between devices: 293 us -> none  [per_device(): summed = lax.psum((grad_wq, grad_wk, grad_wv), 'dp')]
    unnamed x3 -> x0, waiting for transfers between devices: 223 us -> none
    pallas_call x0 -> x2, Pallas kernels: none -> 75.9 us  [the longest x1 71 us: communicate(): pl.pallas_call(comm_kernel, out_shape=(jax.ShapeDtypeStruct((1536, 768),...]
    psum x1 -> x0, blocking collectives: 52.9 us -> none  [per_device(): total = lax.psum(squares(summed), 'head')]
    reduce_sum x3 -> x0, other arithmetic: 8.35 us -> none  [the longest x1 4.15 us: squares(): jnp.sum(grads[0] * grads[0]) + jnp.sum(grads[1] * grads[1])]
    dot_general x6 -> x5, matrix products: 12.1 us -> 12.9 us  [the longest x1 4.23 us: per_device(): grad_wq = jnp.dot(query_latent.T, q_grad, preferred_element_type=F32)]
  transfers between devices with their start and end apart: 2 -> 0, of which waited for: 2 -> 0; matrix products, arithmetic and copies ran while one was open for 1% -> 0% of each run, Pallas kernels for 0% -> 0%
where the time goes in v1:
time: 117 us; the launch traced here: 116 us
  Pallas kernels  75.9 us (65%)
  matrix products  23.3 us (20%)
  local copies, waits for them, and re-layouts  13.5 us (12%)
  other arithmetic  2.78 us (2%)
    pallas_call x1, Pallas kernels, communicate(): pl.pallas_call(comm_kernel, out_shape=(jax.ShapeDtypeStruct((1536, 768),...  71 us
    pallas_call x1, Pallas kernels, finish(): pl.pallas_call(functools.partial(finish_kernel, count), grid=(steps,), ou...  4.85 us
    dot_general x1, matrix products, per_device(): grad_wq = jnp.dot(query_latent.T, q_grad, preferred_element_type=F32)  4.23 us
    dot_general x2, matrix products, attend(): jnp.einsum('hst,thd->shd', probs, values, preferred_element_type=jnp.floa...  4.12 us
    dot_general x3, matrix products, transposed(): lax.dot_general(left, right, (((1,), (1,)), ((), ())), preferred_element_...  3.81 us
    unnamed x46, local copies, waits for them, and re-layouts  3.48 us
    concatenate x1, local copies, waits for them, and re-layouts, per_device(): jnp.concatenate([term_q, term_kv, rot_sum, jnp.zeros((length, LAT - QL -...  3.46 us
    dot_general x1, matrix products, per_device(): jnp.dot(plain_latent.T, jnp.concatenate([key_grad, value_grad], axis=1),...  2.79 us

profile of v1, /device:TPU:2, one launch (start us, length us, event | category | flops | bytes accessed | tf_op | source)
XLA Modules:
  0.0 116.4 jit_solution(4618577519181727342)
XLA Ops:
  0.6 0.0 copy-start
  0.6 0.0 copy-start.10
  0.7 0.9 slice.23
  1.6 0.8 fusion.33
  2.4 1.8 %copy.62 = bf16[256,512]{0,1:T(8,128)(2,1)} copy(bf16[256,512]{1,0:T(8,128)(2,1)} %param.8) | data formatting | bytes 524288 | tf_op jit(solution)/shard_map/reshape | solution.py:411
  4.2 2.1 %convolution_convert_fusion.5 = bf16[256,512]{1,0:T(8,128)(2,1)} fusion(bf16[512,512]{1,0:T(8,128)(2,1)} %param.10, bf16[256,576]{0,1:T(8,128)(2,1)} %param.7), kind=kOutput, calls=%fused_computation.16 | convolution fusion | flops 134348800 | bytes 1048576 | tf_op jit(solution)/shard_map/dot_general | solution.py:399
  6.4 1.1 copy.64
  7.5 0.0 copy-start.8
  7.5 2.3 %fusion.5 = bf16[32,4,8,128]{3,2,1,0:T(8,128)(2,1)} fusion(bf16[512,512]{1,0:T(8,128)(2,1)} %param.11, bf16[256,576]{0,1:T(8,128)(2,1)} %param.7), kind=kOutput, calls=%fused_computation.18 | convolution fusion | flops 134348800 | bytes 1048576 | tf_op jit(solution)/shard_map/dot_general | solution.py:404
  9.7 0.0 copy-done
  9.7 0.0 copy-done.10
  9.7 1.5 %convolution_convert_fusion.1 = bf16[256,768]{1,0:T(8,128)(2,1)} fusion(bf16[256,1536]{1,0:T(8,128)(2,1)S(1)} %copy-done.10, bf16[1536,768]{1,0:T(8,128)(2,1)S(1)} %copy-done), kind=kOutput, calls=%fused_computation.11 | convolution fusion | flops 604176384 | bytes 3538944 | tf_op jit(solution)/shard_map/dot_general | solution.py:395
  11.3 1.2 copy.41
  12.4 0.0 copy-start.6
  12.5 0.0 copy-done.15
  12.5 0.8 subtract_convert_fusion
  13.3 0.0 copy-start.19
  13.3 0.0 copy-start.21
  13.3 0.0 copy-done.8
  13.3 0.3 fusion.24
  13.7 0.0 copy-done.13
  13.7 0.0 copy-done.6
  13.7 0.2 copy-done.19
  13.9 0.0 copy-done.21
  14.0 0.4 fusion.4
  14.3 0.0 copy-start.5
  14.3 1.0 copy-done.5
  15.3 0.7 fusion.38
  16.0 2.7 %convolution_convert_fusion.2 = bf16[4,256,128]{1,2,0:T(8,128)(2,1)} fusion(bf16[4,128,256]{2,1,0:T(8,128)(2,1)} %bitcast.76, f32[4,256]{1,0:T(4,128)S(1)} %get-tuple-element.19, f32[4,256,256]{1,2,0:T(8,128)} %copy-done.5), kind=kOutput, calls=%fused_computation.13 | convolution fusion | flops 68027648 | bytes 1576960 | tf_op jit(solution)/shard_map/transpose(jvp(hst,thd->shd))/dot_general | solution.py:57
  18.8 0.0 copy-start.22
  18.8 1.4 %fusion.18 = (f32[4,256]{1,0:T(4,128)S(1)}, bf16[4,256,256]{2,1,0:T(8,128)(2,1)S(1)}) fusion(f32[4,256,256]{1,2,0:T(8,128)S(1)} %get-tuple-element.20, f32[4,256]{1,0:T(4,128)S(1)} %multiply_divide_fusion, bf16[4,128,256]{2,1,0:T(8,128)(2,1)} %bitcast.77, bf16[32,4,8,128]{3,2,1,0:T(8,128)(2,1)} %fusion.5), kind=kOutput, calls=%fused_computation.33 | convolution fusion | flops 68418560 | bytes 2105344 | tf_op jit(solution)/shard_map/transpose(jvp(hst,thd->shd))/dot_general | solution.py:57
  20.2 0.0 copy-start.9
  20.2 0.0 copy-start.14
  20.2 0.2 fusion.15
  20.5 0.0 copy-done.7
  20.5 0.0 copy-start.16
  20.5 0.0 copy-start.17
  20.5 0.3 convolution_convert_fusion.3
  20.8 0.0 copy-done.20
  20.8 0.0 copy-done.22
  20.8 0.0 copy-start.12
  20.9 0.9 fusion.10
  21.8 0.0 copy-done.9
  21.8 0.2 fusion.6
  22.0 0.0 copy-done.14
  22.0 0.2 fusion.9
  22.2 0.0 copy-done.16
  22.2 0.0 copy-done.17
  22.4 1.6 %copy.53 = f32[256,64]{1,0:T(8,128)} copy(f32[256,64]{0,1:T(8,128)} %fusion.10) | data formatting | bytes 131072 | tf_op jit(solution)/shard_map/reduce_sum | solution.py:416
  24.0 0.0 copy-done.12
  24.0 0.3 fusion.40
  24.3 1.5 %convolution_add_fusion.1 = f32[256,512]{1,0:T(8,128)S(1)} fusion(f32[256,512]{1,0:T(8,128)S(1)} %fusion.40, bf16[256,512]{0,1:T(8,128)(2,1)} %bitcast.74, bf16[512,512]{1,0:T(8,128)(2,1)} %param.11), kind=kOutput, calls=%fused_computation.12 | convolution fusion | flops 134348800 | bytes 1835008 | tf_op jit(solution)/shard_map/dot_general | solution.py:61
  25.8 0.0 copy-done.18
  25.8 2.8 %convolution_bitcast_fusion.1.kv_ref = f32[512,1024]{1,0:T(8,128)} fusion(bf16[256,512]{0,1:T(8,128)(2,1)} %bitcast.75, bf16[256,512]{0,1:T(8,128)(2,1)S(1)} %bitcast.73, bf16[256,576]{0,1:T(8,128)(2,1)S(1)} %copy-done.18), kind=kOutput, calls=%fused_computation.2 | convolution fusion | flops 269484032 | bytes 2883584 | tf_op jit(solution)/shard_map/dot_general | solution.py:423
  28.6 2.0 %fusion.39 = f32[256,1536]{1,0:T(8,128)} fusion(bf16[256,768]{0,1:T(8,128)(2,1)S(1)} %bitcast.65, bf16[1536,768]{1,0:T(8,128)(2,1)S(1)} %copy-done), kind=kOutput, calls=%fused_computation.67 | convolution fusion | flops 603979776 | bytes 4325376 | tf_op jit(solution)/shard_map/dot_general | solution.py:61
  30.6 0.0 copy-done.11
  30.6 3.5 %concatenate.16 = f32[256,2176]{1,0:T(8,128)} concatenate(f32[256,1536]{1,0:T(8,128)} %fusion.39, f32[256,512]{1,0:T(8,128)S(1)} %convolution_add_fusion.1, f32[256,64]{1,0:T(8,128)S(1)} %copy-done.11, f32[256,64]{1,0:T(8,128)S(1)} %broadcast_in_dim.48), dimensions={1} | concatenate | bytes 4456448 | tf_op jit(solution)/shard_map/concatenate | solution.py:419
  34.1 4.2 %convolution_bitcast_fusion.q_ref = f32[1536,768]{1,0:T(8,128)} fusion(bf16[256,768]{0,1:T(8,128)(2,1)S(1)} %bitcast.66, bf16[256,1536]{1,0:T(8,128)(2,1)} %param.6), kind=kOutput, calls=%fused_computation.1 | convolution fusion | flops 603979776 | bytes 5898240 | tf_op jit(solution)/shard_map/dot_general | solution.py:422
  38.3 0.0 copy-done.1
  38.3 71.0 %comm.1 = (bf16[1536,768]{1,0:T(8,128)(2,1)}, bf16[512,1024]{1,0:T(8,128)(2,1)S(1)}, f32[8,8,128]{2,1,0:T(8,128)S(1)}, f32[8,2176]{1,0:T(8,128)S(1)}) custom-call(f32[1536,768]{1,0:T(8,128)} %convolution_bitcast_fusion.q_ref, f32[512,1024]{1,0:T(8,128)S(1)} %copy-done.1, f32[16,2,8,2176]{3,2,1,0:T(8,128)} %bitcast.64), custom_call_target="tpu_custom_call" | custom-call | tf_op jit(solution)/shard_map/comm/pallas_call | solution.py:330
  109.4 1.0 copy-done.2
  110.3 0.6 copy-done.3
  110.9 0.6 copy-done.4
  111.5 4.8 %finish.1 = (f32[8,1536]{1,0:T(8,128)}, f32[8,576]{1,0:T(8,128)}, bf16[1536,768]{1,0:T(8,128)(2,1)}, bf16[512,512]{1,0:T(8,128)(2,1)}, bf16[512,512]{1,0:T(8,128)(2,1)}) custom-call(f32[8,8,128]{2,1,0:T(8,128)} %copy-done.4, f32[8,2176]{1,0:T(8,128)} %copy-done.3, bf16[1536,768]{1,0:T(8,128)(2,1)} %get-tuple-element.11.q_ref, bf16[512,1024]{1,0:T(8,128)(2,1)} %copy-done.2), custom_call_target="tpu_custom_call" | custom-call | tf_op jit(solution)/shard_map/finish/pallas_call | solution.py:365
  (19 shorter events, 0.2 us)
Async XLA Ops:
  0.6 9.1 %copy-start = (bf16[1536,768]{1,0:T(8,128)(2,1)S(1)}, bf16[1536,768]{1,0:T(8,128)(2,1)}, u32[]{:S(2)}) copy-start(bf16[1536,768]{1,0:T(8,128)(2,1)} %param.9) | copy-start | bytes 7077892
  0.6 9.1 %copy-start.10 = (bf16[256,1536]{1,0:T(8,128)(2,1)S(1)}, bf16[256,1536]{1,0:T(8,128)(2,1)}, u32[]{:S(2)}) copy-start(bf16[256,1536]{1,0:T(8,128)(2,1)} %param.6) | copy-start | bytes 2359300
  1.6 12.1 %copy-start.13 = (bf16[256,64]{0,1:T(8,128)(2,1)}, bf16[256,64]{0,1:T(8,128)(2,1)S(1)}, u32[]{:S(2)}) copy-start(bf16[256,64]{0,1:T(8,128)(2,1)S(1)} %slice.23) | copy-start | bytes 98308
  2.4 10.1 %copy-start.15 = (f32[256,32]{0,1:T(8,128)}, f32[256,32]{0,1:T(8,128)S(1)}, u32[]{:S(2)}) copy-start(f32[256,32]{0,1:T(8,128)S(1)} %get-tuple-element.17) | copy-start | bytes 98308
  7.5 5.9 %copy-start.8 = (bf16[256,512]{0,1:T(8,128)(2,1)}, bf16[256,512]{0,1:T(8,128)(2,1)S(1)}, u32[]{:S(2)}) copy-start(bf16[256,512]{0,1:T(8,128)(2,1)S(1)} %copy.64) | copy-start | bytes 786436
  12.4 1.3 %copy-start.6 = (bf16[256,768]{0,1:T(8,128)(2,1)}, bf16[256,768]{0,1:T(8,128)(2,1)S(1)}, u32[]{:S(2)}) copy-start(bf16[256,768]{0,1:T(8,128)(2,1)S(1)} %copy.41) | copy-start | bytes 1179652
  13.3 0.6 copy-start.19
  13.3 0.6 copy-start.21
  14.3 1.0 copy-start.5
  18.8 1.7 %copy-start.7 = (bf16[256,768]{0,1:T(8,128)(2,1)S(1)}, bf16[256,768]{0,1:T(8,128)(2,1)}, u32[]{:S(2)}) copy-start(bf16[256,768]{0,1:T(8,128)(2,1)} %copy-done.6) | copy-start | bytes 1179652
  18.8 2.0 %copy-start.20 = (bf16[256,4,32]{0,2,1:T(8,128)(2,1)S(1)}, bf16[256,4,32]{0,2,1:T(8,128)(2,1)}, u32[]{:S(2)}) copy-start(bf16[256,4,32]{0,2,1:T(8,128)(2,1)} %copy-done.19) | copy-start | bytes 196612
  18.8 2.0 %copy-start.22 = (bf16[256,4,32]{0,2,1:T(8,128)(2,1)S(1)}, bf16[256,4,32]{0,2,1:T(8,128)(2,1)}, u32[]{:S(2)}) copy-start(bf16[256,4,32]{0,2,1:T(8,128)(2,1)} %copy-done.21) | copy-start | bytes 196612
  20.2 1.6 %copy-start.9 = (bf16[256,512]{0,1:T(8,128)(2,1)S(1)}, bf16[256,512]{0,1:T(8,128)(2,1)}, u32[]{:S(2)}) copy-start(bf16[256,512]{0,1:T(8,128)(2,1)} %copy-done.8) | copy-start | bytes 786436
  20.2 1.8 %copy-start.14 = (bf16[256,64]{0,1:T(8,128)(2,1)S(1)}, bf16[256,64]{0,1:T(8,128)(2,1)}, u32[]{:S(2)}) copy-start(bf16[256,64]{0,1:T(8,128)(2,1)} %copy-done.13) | copy-start | bytes 98308
  20.5 1.8 %copy-start.16 = (f32[256,32]{0,1:T(8,128)S(1)}, f32[256,32]{0,1:T(8,128)}, u32[]{:S(2)}) copy-start(f32[256,32]{0,1:T(8,128)} %copy-done.15) | copy-start | bytes 98308
  20.5 1.8 %copy-start.17 = (f32[256,32]{0,1:T(8,128)S(1)}, f32[256,32]{0,1:T(8,128)}, u32[]{:S(2)}) copy-start(f32[256,32]{0,1:T(8,128)} %get-tuple-element.18) | copy-start | bytes 98308
  20.8 3.1 %copy-start.12 = (bf16[512,512]{1,0:T(8,128)(2,1)S(1)}, bf16[512,512]{1,0:T(8,128)(2,1)}, u32[]{:S(2)}) copy-start(bf16[512,512]{1,0:T(8,128)(2,1)} %param.10) | copy-start | bytes 1572868
  24.0 1.8 %copy-start.18 = (bf16[256,576]{0,1:T(8,128)(2,1)S(1)}, bf16[256,576]{0,1:T(8,128)(2,1)}, u32[]{:S(2)}) copy-start(bf16[256,576]{0,1:T(8,128)(2,1)} %param.7) | copy-start | bytes 884740
  28.6 2.0 %copy-start.11 = (f32[256,64]{1,0:T(8,128)S(1)}, f32[256,64]{1,0:T(8,128)}, u32[]{:S(2)}) copy-start(f32[256,64]{1,0:T(8,128)} %copy.53) | copy-start | bytes 196612
  34.1 4.2 %copy-start.1 = (f32[512,1024]{1,0:T(8,128)S(1)}, f32[512,1024]{1,0:T(8,128)}, u32[]{:S(2)}) copy-start(f32[512,1024]{1,0:T(8,128)} %convolution_bitcast_fusion.1.kv_ref) | copy-start | bytes 6291460
  109.3 1.0 copy-start.2
  110.3 0.6 copy-start.3
  110.9 0.6 copy-start.4

commit v2 on v0

v2 whole, which is shorter than its diff:
```python
import functools

import jax
import jax.numpy as jnp
import numpy as np
from jax import lax
from jax.experimental import pallas as pl
from jax.experimental.pallas import tpu as pltpu
from jax.sharding import PartitionSpec as P

QL = 1536
KL = 512
DN = 128
DR = 64
DQ = DN + DR
ROWS = 256
HEADS = 4
LAT = 2176

max_rms = 1.0
eps = 1e-06

MESH = pl.DeviceIdType.MESH
BF = jnp.bfloat16
F32 = jnp.float32

PIECES = (
    ("v", 0, 0, 512, 512, "XAB"),
    ("q", 0, 0, 768, 384, "ABX"),
    ("q", 768, 0, 768, 384, "BXA"),
    ("k", 0, 0, 512, 512, "XAB"),
    ("q", 0, 384, 768, 384, "ABX"),
    ("q", 768, 384, 768, 384, "BXA"),
)
N = len(PIECES)
CHUNK = 32


def tables():
    half = DR // 2
    freqs = np.float32(10000.0) ** (np.float32(-2.0) * np.arange(half, dtype=np.float32) / DR)
    angle = np.arange(ROWS, dtype=np.float32)[:, None] * freqs.astype(np.float32)[None, :]
    cosine, sine = np.cos(angle), np.sin(angle)
    swap = np.zeros((DR, DR), np.float32)
    for i in range(half):
        swap[half + i, i] = -1.0
        swap[i, half + i] = 1.0
    trig = np.stack([np.concatenate([t, t], axis=1) for t in (cosine, sine)])
    return trig.astype(np.float32), swap


def for_rows(rows, step, body):
    def one(i, carry):
        body(pl.multiple_of(i * step, step))
        return carry

    lax.fori_loop(0, rows // step, one, 0)


def places():
    d, h = lax.axis_index("dp"), lax.axis_index("head")
    y, xh = d // 2, d % 2
    b, y0 = y // 2, y % 2
    a = (y0 + b) % 2
    z, r = h // 4, h % 4
    xl, c = r // 2, r % 2
    bits = {"A": a, "B": b, "X": xh}
    peer = {
        "A": (2 * (y + 1 - 2 * y0) + xh, h),
        "B": (2 * (3 - y) + xh, h),
        "X": (2 * y + 1 - xh, h),
        "C": (d, h + 1 - 2 * c),
        "L": (d, h + 2 - 4 * xl),
    }
    for k in range(1, 8):
        peer["Z%d" % k] = (d, (h + 4 * k) % 32)
    return bits, peer, z, xl, c


def dot(left, right):
    return jnp.dot(left, right, preferred_element_type=F32)


def dot_nt(left, right):
    return lax.dot_general(left, right, (((1,), (1,)), ((), ())), preferred_element_type=F32)


def dot_tn(left, right):
    return lax.dot_general(left, right, (((0,), (0,)), ((), ())), preferred_element_type=F32)


def step_kernel(
    ql_hbm, kvl_hbm, dy_hbm, wq_hbm, wk_hbm, wv_hbm, trig_hbm, swap_hbm,
    g0, g1, g2, g3, g4, g5, s_out, lat_out,
    ql, kvlt, dy, wq, wk, wv, trig, swap,
    qlt, dqs, dks, dvs,
    stg0, stg1, stg2, stg3, stg4, stg5,
    rcv0, rcv1, rcv2, rcv3, rcv4, rcv5,
    ra0, ra1, ra2, ra3, ra4, ra5,
    rb0, rb1, rb2, rb3, rb4, rb5,
    lat, lrecv, lsum, zs, zr, lx, lxr,
    sv, sr, sz,
    in_sem, rs_send, rs_recv, ag_send, ag_recv, l_send, l_recv, s_send, s_recv,
):
    loads = [
        pltpu.make_async_copy(src, dst, in_sem.at[i])
        for i, (src, dst) in enumerate((
            (kvl_hbm, kvlt), (wk_hbm, wk), (wv_hbm, wv), (ql_hbm, ql), (wq_hbm, wq),
            (dy_hbm, dy), (trig_hbm, trig), (swap_hbm, swap),
        ))
    ]
    for load in loads:
        load.start()
    bits, peer, z, xl, c = places()
    barrier = pltpu.get_barrier_semaphore()
    for where in peer.values():
        pl.semaphore_signal(barrier, inc=1, device_id=where, device_id_type=MESH)

    g = (g0, g1, g2, g3, g4, g5)
    stg = (stg0, stg1, stg2, stg3, stg4, stg5)
    rcv = (rcv0, rcv1, rcv2, rcv3, rcv4, rcv5)
    red = ((ra0, rb0), (ra1, rb1), (ra2, rb2), (ra3, rb3), (ra4, rb4), (ra5, rb5))

    for load in loads[:3]:
        load.wait()
    plain = jnp.transpose(kvlt[:KL, :])
    key_rot = jnp.transpose(kvlt[KL:, :])
    keys = dot(plain, wk[...]).astype(BF)
    values = dot(plain, wv[...]).astype(BF)
    for load in loads[3:]:
        load.wait()
    queries = dot(ql[...], wq[...]).astype(BF)
    qlt[...] = jnp.transpose(ql[...])

    scale = 1.0 / DQ**0.5
    allowed = lax.broadcasted_iota(jnp.int32, (ROWS, ROWS), 0) <= lax.broadcasted_iota(
        jnp.int32, (ROWS, ROWS), 1
    )
    cosine, sine = trig[0], trig[1]
    turn = swap[...]
    rot = jnp.zeros((ROWS, DR), F32)
    parts = []
    for n in range(HEADS):
        q_plain = queries[:, DQ * n : DQ * n + DN]
        q_rot = queries[:, DQ * n + DN : DQ * (n + 1)]
        q_rope = (q_rot.astype(F32) * cosine + dot(q_rot, turn) * sine).astype(BF)
        key = keys[:, DN * n : DN * (n + 1)]
        value = values[:, DN * n : DN * (n + 1)]
        grad = dy[:, DN * n : DN * (n + 1)]
        q_all = jnp.concatenate([q_plain, q_rope], axis=1)
        k_all = jnp.concatenate([key, key_rot], axis=1)
        scores = jnp.where(allowed, dot_nt(k_all, q_all) * scale, -jnp.inf)
        top = jnp.max(scores, axis=0, keepdims=True)
        weights = jnp.exp(scores - top)
        probs = weights / jnp.sum(weights, axis=0, keepdims=True)
        dvs[:, DN * n : DN * (n + 1)] = dot(probs.astype(BF), grad).astype(BF)
        dp = dot_nt(value, grad)
        mean = jnp.sum(dp * probs, axis=0, keepdims=True)
        ds = (probs * (dp - mean) * scale).astype(BF)
        dk = dot(ds, q_all)
        dks[:, DN * n : DN * (n + 1)] = dk[:, :DN].astype(BF)
        rot = rot + dk[:, DN:].astype(BF).astype(F32)
        dq = dot_tn(ds, k_all)
        d_rope = dq[:, DN:].astype(BF)
        d_rot = d_rope.astype(F32) * cosine + dot_nt(d_rope, turn) * sine
        parts.append(jnp.concatenate([dq[:, :DN].astype(BF), d_rot.astype(BF)], axis=1))
        if n % 2:
            dqs[:, DQ * (n - 1) : DQ * (n + 1)] = jnp.concatenate(parts, axis=1)
            parts = []

    def remote(src, dst, send, recv, where):
        copy = pltpu.make_async_remote_copy(
            src_ref=src, dst_ref=dst, send_sem=send, recv_sem=recv,
            device_id=peer[where], device_id_type=MESH,
        )
        copy.start()
        return copy

    def product(p, lo, n):
        which, r0, c0, _, cols, _ = PIECES[p]
        if which == "q":
            return dot(qlt[pl.ds(r0 + lo, n), :], dqs[:, c0 : c0 + cols])
        return dot(kvlt[pl.ds(lo, n), :], (dks if which == "k" else dvs)[...])

    def area(p, s):
        rows = PIECES[p][3]
        return (0, rows // 2, rows // 2 + rows // 4)[s], rows >> (s + 1)

    def rs_send_off(p, s):
        off, n = area(p, s)
        return remote(
            stg[p].at[pl.ds(off, n)], rcv[p].at[pl.ds(off, n)],
            rs_send.at[p, s], rs_recv.at[p, s], PIECES[p][5][s],
        )

    def rs_first(p):
        off, n = area(p, 0)
        away = pl.multiple_of((1 - bits[PIECES[p][5][0]]) * n, 128)
        for i in range(0, n, 128):
            stg[p][i : i + 128, :] = product(p, away + i, 128).astype(BF)
        return rs_send_off(p, 0)

    def rs_keep(p):
        off, n = area(p, 0)
        keep = pl.multiple_of(bits[PIECES[p][5][0]] * n, 128)
        for i in range(0, n, 128):
            red[p][0][i : i + 128, :] = product(p, keep + i, 128)

    def rs_second(p, copy):
        copy.wait()
        off, n = area(p, 1)
        bit = bits[PIECES[p][5][1]]
        away, keep = (1 - bit) * n, bit * n

        def total(lo):
            return red[p][0][pl.ds(lo, CHUNK), :] + rcv[p][pl.ds(lo, CHUNK), :].astype(F32)

        def out(i):
            stg[p][pl.ds(off + i, CHUNK), :] = total(pl.multiple_of(away + i, CHUNK)).astype(BF)

        for_rows(n, CHUNK, out)
        sent = rs_send_off(p, 1)

        def hold(i):
            red[p][1][pl.ds(i, CHUNK), :] = total(pl.multiple_of(keep + i, CHUNK))

        for_rows(n, CHUNK, hold)
        return sent

    def rs_third(p, copy):
        copy.wait()
        before, _ = area(p, 1)
        off, n = area(p, 2)
        bit = bits[PIECES[p][5][2]]
        away = (1 - bit) * n

        def out(i):
            lo = pl.multiple_of(away + i, CHUNK)
            stg[p][pl.ds(off + i, CHUNK), :] = (
                red[p][1][pl.ds(lo, CHUNK), :]
                + rcv[p][pl.ds(pl.multiple_of(before + lo, CHUNK), CHUNK), :].astype(F32)
            ).astype(BF)

        for_rows(n, CHUNK, out)
        return rs_send_off(p, 2)

    def owned(p, s):
        rows, order = PIECES[p][3], PIECES[p][5]
        lo = 0
        for t in range(s + 1):
            lo = lo + bits[order[t]] * (rows >> (t + 1))
        return pl.multiple_of(lo, CHUNK)

    def rs_last(p, copy):
        copy.wait()
        before, _ = area(p, 1)
        off, n = area(p, 2)
        keep = bits[PIECES[p][5][2]] * n
        lo = owned(p, 2)

        def body(i):
            at = pl.multiple_of(keep + i, CHUNK)
            total = (
                red[p][1][pl.ds(at, CHUNK), :]
                + rcv[p][pl.ds(pl.multiple_of(before + at, CHUNK), CHUNK), :].astype(F32)
                + rcv[p][pl.ds(off + i, CHUNK), :].astype(F32)
            )
            g[p][pl.ds(pl.multiple_of(lo + i, CHUNK), CHUNK), :] = total.astype(BF)
            square = total * total
            part = square[:, :128]
            for j in range(1, PIECES[p][4] // 128):
                part = part + square[:, 128 * j : 128 * (j + 1)]
            sv[0] = sv[0] + part[:8] + part[8:16] + part[16:24] + part[24:32]

        for_rows(n, CHUNK, body)

    def ag_start(p, s):
        block = g[p].at[pl.ds(owned(p, s), PIECES[p][3] >> (s + 1))]
        return remote(block, block, ag_send.at[p, s], ag_recv.at[p, s], PIECES[p][5][s])

    pl.semaphore_wait(barrier, len(peer))
    first = [rs_first(p) for p in range(N)]
    for p in range(N):
        rs_keep(p)

    lat[:, :, :, :QL] = dot_nt(dqs[...], wq[...]).reshape(16, 2, 8, QL)
    lat[:, :, :, QL : QL + KL] = (dot_nt(dks[...], wk[...]) + dot_nt(dvs[...], wv[...])).reshape(
        16, 2, 8, KL
    )
    lat[:, :, :, QL + KL :] = jnp.concatenate([rot, jnp.zeros((ROWS, DR), F32)], axis=1).reshape(
        16, 2, 8, 128
    )
    core = remote(lat.at[:, 1 - c], lrecv, l_send.at[0], l_recv.at[0], "C")
    second = [None] * N
    for p in range(3):
        second[p] = rs_second(p, first[p])
    core.wait()

    def core_body(k, carry):
        lsum[k] = lat[k, c] + lrecv[k]
        return carry

    lax.fori_loop(0, 16, core_body, 0)

    def zs_body(k, carry):
        zs[k] = jnp.concatenate([lsum[2 * k], lsum[2 * k + 1]], axis=0).astype(BF)
        return carry

    lax.fori_loop(0, 8, zs_body, 0)
    zcopies = [
        remote(zs.at[(z + k) % 8], zr.at[k - 1], l_send.at[k], l_recv.at[k], "Z%d" % k)
        for k in range(1, 8)
    ]
    for p in range(3, N):
        second[p] = rs_second(p, first[p])
    third = [rs_third(p, second[p]) for p in range(N)]
    sv[0] = jnp.zeros((8, 128), F32)
    gather = []
    for p in range(N):
        rs_last(p, third[p])
        gather.append(ag_start(p, 2))

    def s_step(i, dim):
        return remote(sv.at[i], sr.at[i], s_send.at[i], s_recv.at[i], dim)

    def s_add(copy, i):
        copy.wait()
        sv[i + 1] = sv[i] + sr[i]

    s0 = s_step(0, "A")
    s_add(s0, 0)
    s1 = s_step(1, "C")
    s_add(s1, 1)
    s2 = s_step(2, "B")
    later = []
    for p in range(N):
        gather[p].wait()
        later.append(ag_start(p, 1))
    s_add(s2, 2)
    s3 = s_step(3, "L")
    for copy in zcopies:
        copy.wait()
    lx[0] = lsum[2 * z]
    lx[1] = lsum[2 * z + 1]
    for k in range(7):
        got = zr[k].astype(F32)
        lx[0] = lx[0] + got[:8]
        lx[1] = lx[1] + got[8:]
    xcopy = remote(lx.at[1 - xl], lxr, l_send.at[8], l_recv.at[8], "L")
    s_add(s3, 3)
    s4 = s_step(4, "X")
    last = []
    for p in range(N):
        later[p].wait()
        last.append(ag_start(p, 0))
    s_add(s4, 4)
    szc = [
        remote(sv.at[5], sz.at[z], s_send.at[4 + k], s_recv.at[4 + k], "Z%d" % k)
        for k in range(1, 8)
    ]
    sz[z] = sv[5]
    xcopy.wait()
    lat_out[...] = lx[xl] + lxr[...]
    for copy in szc:
        copy.wait()
    s_out[...] = sz[...]
    for copy in last:
        copy.wait()


def step(ql, kvl, dy, wq, wk, wv):
    trig, swap = tables()
    vmem = pl.BlockSpec(memory_space=pltpu.VMEM)
    hbm = pl.BlockSpec(memory_space=pltpu.HBM)

    def moved(p):
        rows = PIECES[p][3]
        return rows // 2 + rows // 4 + rows // 8

    scratch = [
        pltpu.VMEM((ROWS, QL), BF),
        pltpu.VMEM((KL + DR, ROWS), BF),
        pltpu.VMEM((ROWS, HEADS * DN), BF),
        pltpu.VMEM((QL, HEADS * DQ), BF),
        pltpu.VMEM((KL, HEADS * DN), BF),
        pltpu.VMEM((KL, HEADS * DN), BF),
        pltpu.VMEM((2, ROWS, DR), F32),
        pltpu.VMEM((DR, DR), BF),
        pltpu.VMEM((QL, ROWS), BF),
        pltpu.VMEM((ROWS, HEADS * DQ), BF),
        pltpu.VMEM((ROWS, HEADS * DN), BF),
        pltpu.VMEM((ROWS, HEADS * DN), BF),
    ]
    scratch += [pltpu.VMEM((moved(p), PIECES[p][4]), BF) for p in range(N)] * 2
    scratch += [pltpu.VMEM((PIECES[p][3] // 2, PIECES[p][4]), F32) for p in range(N)]
    scratch += [pltpu.VMEM((PIECES[p][3] // 4, PIECES[p][4]), F32) for p in range(N)]
    scratch += [
        pltpu.VMEM((16, 2, 8, LAT), F32),
        pltpu.VMEM((16, 8, LAT), F32),
        pltpu.VMEM((16, 8, LAT), F32),
        pltpu.VMEM((8, 16, LAT), BF),
        pltpu.VMEM((7, 16, LAT), BF),
        pltpu.VMEM((2, 8, LAT), F32),
        pltpu.VMEM((8, LAT), F32),
        pltpu.VMEM((6, 8, 128), F32),
        pltpu.VMEM((5, 8, 128), F32),
        pltpu.VMEM((8, 8, 128), F32),
    ]
    dma = pltpu.SemaphoreType.DMA
    scratch += [dma((8,)), dma((N, 3)), dma((N, 3)), dma((N, 3)), dma((N, 3))]
    scratch += [dma((9,)), dma((9,)), dma((12,)), dma((12,))]
    return pl.pallas_call(
        step_kernel,
        out_shape=tuple(jax.ShapeDtypeStruct((p[3], p[4]), BF) for p in PIECES)
        + (jax.ShapeDtypeStruct((8, 8, 128), F32), jax.ShapeDtypeStruct((8, LAT), F32)),
        in_specs=[hbm] * 8,
        out_specs=(vmem,) * (N + 2),
        scratch_shapes=scratch,
        name="step",
        compiler_params=pltpu.CompilerParams(
            collective_id=0, has_side_effects=True, vmem_limit_bytes=46 << 20
        ),
    )(*(pltpu.with_memory_space_constraint(t, pltpu.HBM) for t in (ql, kvl, dy, wq, wk, wv, jnp.asarray(trig), jnp.asarray(swap, BF))))


def finish_kernel(
    count, s_ref, lat_ref, g0, g1, g2, g3, g4, g5,
    ql_out, kvl_out, q_out, k_out, v_out,
    b0, b1, b2, b3, b4, b5, kvl, sem,
):
    kvl[...] = lat_ref[:, QL : QL + KL + DR]
    copies = [
        pltpu.make_async_copy(lat_ref.at[:, pl.ds(0, QL)], ql_out, sem.at[N]),
        pltpu.make_async_copy(kvl, kvl_out, sem.at[N + 1]),
    ]
    for copy in copies:
        copy.start()
    total = jnp.sum(s_ref[...], axis=0)
    total = jnp.sum(total, axis=0, keepdims=True)
    total = jnp.sum(total, axis=1, keepdims=True)
    factor = jnp.minimum(1.0, max_rms * count**0.5 / jnp.sqrt(total + eps))
    for p, (src, buf) in enumerate(zip((g0, g1, g2, g3, g4, g5), (b0, b1, b2, b3, b4, b5))):
        which, r0, c0, rows, cols, _ = PIECES[p]

        def body(i):
            buf[pl.ds(i, CHUNK), :] = (src[pl.ds(i, CHUNK), :].astype(F32) * factor).astype(BF)

        for_rows(rows, CHUNK, body)
        if which == "q":
            dst = q_out.at[pl.ds(r0, rows), pl.ds(c0, cols)]
        else:
            dst = k_out if which == "k" else v_out
        copy = pltpu.make_async_copy(buf, dst, sem.at[p])
        copy.start()
        copies.append(copy)
    for copy in copies:
        copy.wait()


def finish(count, s, lat, pieces):
    vmem = pl.BlockSpec(memory_space=pltpu.VMEM)
    hbm = pl.BlockSpec(memory_space=pl.ANY)
    return pl.pallas_call(
        functools.partial(finish_kernel, count),
        out_shape=(
            jax.ShapeDtypeStruct((8, QL), F32),
            jax.ShapeDtypeStruct((8, KL + DR), F32),
            jax.ShapeDtypeStruct((QL, HEADS * DQ), BF),
            jax.ShapeDtypeStruct((KL, HEADS * DN), BF),
            jax.ShapeDtypeStruct((KL, HEADS * DN), BF),
        ),
        in_specs=[vmem] * (N + 2),
        out_specs=(hbm,) * 5,
        scratch_shapes=[pltpu.VMEM((p[3], p[4]), BF) for p in PIECES]
        + [pltpu.VMEM((8, KL + DR), F32), pltpu.SemaphoreType.DMA((N + 2,))],
        name="finish",
        compiler_params=pltpu.CompilerParams(vmem_limit_bytes=16 << 20),
    )(s, lat, *pieces)


def per_device(query_latent, kv_latent, out_grad, query_up, key_up, value_up):
    width = lax.axis_size("head")
    count = (QL * query_up.shape[1] + 2 * KL * key_up.shape[1]) * width
    *pieces, s, lat = step(query_latent, kv_latent.T, out_grad, query_up, key_up, value_up)
    return tuple(finish(count, s, lat, pieces))


def solution(mesh):
    placed = (
        P("dp", None),
        P("dp", None),
        P("dp", "head"),
        P(None, "head"),
        P(None, "head"),
        P(None, "head"),
    )
    return jax.shard_map(
        per_device,
        mesh=mesh,
        in_specs=placed,
        out_specs=(
            P(("dp", "head"), None),
            P(("dp", "head"), None),
            P(None, "head"),
            P(None, "head"),
            P(None, "head"),
        ),
        check_vma=False,
    )
```

time: 644 us -> 68.6 us (0.11)
  waiting for transfers between devices: 515 us -> 0 us
  Pallas kernels: 0 us -> 67.8 us
  blocking collectives: 52.9 us -> 0 us
  matrix products: 20.5 us -> 0 us
  other arithmetic: 17.3 us -> 0 us
  between operations: 17.7 us -> 0.64 us
  local copies, waits for them, and re-layouts: 15.4 us -> 0 us
    psum x1 -> x0, waiting for transfers between devices: 293 us -> none  [per_device(): summed = lax.psum((grad_wq, grad_wk, grad_wv), 'dp')]
    unnamed x3 -> x0, waiting for transfers between devices: 223 us -> none
    pallas_call x0 -> x2, Pallas kernels: none -> 67.8 us  [the longest x1 65.5 us: step(): pl.pallas_call(step_kernel, out_shape=tuple((jax.ShapeDtypeStruct((p[3],...]
    psum x1 -> x0, blocking collectives: 52.9 us -> none  [per_device(): total = lax.psum(squares(summed), 'head')]
    dot_general x17 -> x0, matrix products: 20.5 us -> none  [the longest x2 4.11 us: attend(): jnp.einsum('hst,thd->shd', probs, values, preferred_element_type=jnp.floa...]
    unnamed x42 -> x0, local copies, waits for them, and re-layouts: 9.48 us -> none
    reduce_sum x3 -> x0, other arithmetic: 8.35 us -> none  [the longest x1 4.15 us: squares(): jnp.sum(grads[0] * grads[0]) + jnp.sum(grads[1] * grads[1])]
  transfers between devices with their start and end apart: 2 -> 0, of which waited for: 2 -> 0; matrix products, arithmetic and copies ran while one was open for 1% -> 0% of each run, Pallas kernels for 0% -> 0%
where the time goes in v2:
time: 68.6 us; the launch traced here: 68.5 us
  Pallas kernels  67.8 us (99%)
    pallas_call x1, Pallas kernels, step(): pl.pallas_call(step_kernel, out_shape=tuple((jax.ShapeDtypeStruct((p[3],...  65.5 us
    pallas_call x1, Pallas kernels, finish(): pl.pallas_call(functools.partial(finish_kernel, count), out_shape=(jax.Sh...  2.34 us

profile of v2, /device:TPU:2, one launch (start us, length us, event | category | flops | bytes accessed | tf_op | source)
XLA Modules:
  0.0 68.5 jit_solution(6802964435694972002)
XLA Ops:
  0.6 65.5 %step.1 = (bf16[512,512]{1,0:T(8,128)(2,1)S(1)}, bf16[768,384]{1,0:T(8,128)(2,1)S(1)}, bf16[768,384]{1,0:T(8,128)(2,1)S(1)}, bf16[512,512]{1,0:T(8,128)(2,1)S(1)...) custom-call(bf16[256,1536]{1,0:T(8,128)(2,1)} %ql_hbm.1, ...), custom_call_target="tpu_custom_call" | custom-call | tf_op jit(solution)/shard_map/step/pallas_call | solution.py:412
  66.2 2.3 %finish.1 = (f32[8,1536]{1,0:T(8,128)}, f32[8,576]{1,0:T(8,128)}, bf16[1536,768]{1,0:T(8,128)(2,1)}, bf16[512,512]{1,0:T(8,128)(2,1)}, bf16[512,512]{1,0:T(8,128)(2,1)}) custom-call(f32[8,8,128]{2,1,0:T(8,128)S(1)} %get-tuple-element.13.s_ref, f32[8,2176]{1,0:T(8,128)S(1)} %get-tuple-element.14.lat_ref, bf16[512,512]{1,0:T(8,128)(2,1)S(1)} %get-tuple-element.15.g0, ...), custom_call_target="tpu_custom_call" | custom-call | tf_op jit(solution)/shard_map/finish/pallas_call | solution.py:463

commit v3 on v2

v3 whole, which is shorter than its diff:
```python
import functools

import jax
import jax.numpy as jnp
import numpy as np
from jax import lax
from jax.experimental import pallas as pl
from jax.experimental.pallas import tpu as pltpu
from jax.sharding import PartitionSpec as P

QL = 1536
KL = 512
DN = 128
DR = 64
DQ = DN + DR
ROWS = 256
HEADS = 4
LAT = 2176

max_rms = 1.0
eps = 1e-06

MESH = pl.DeviceIdType.MESH
BF = jnp.bfloat16
F32 = jnp.float32

PAIRS = 2
QC = 2 * DQ
KC = 4 * DN
SHAPES = ((768, QC), (768, QC), (512, KC))
G = PAIRS * len(SHAPES)
ORDERS = ("ABX", "BXA", "XAB")
SUB = 2
PIECES = tuple(
    (3 * j + kind, kind, SHAPES[kind][0] // SUB * u, SHAPES[kind][0] // SUB)
    for j in range(PAIRS)
    for u in range(SUB)
    for kind in range(3)
)
N = len(PIECES)
STEPS = (48, 48, 32)


def tables():
    half = DR // 2
    freqs = np.float32(10000.0) ** (np.float32(-2.0) * np.arange(half, dtype=np.float32) / DR)
    angle = np.arange(ROWS, dtype=np.float32)[:, None] * freqs.astype(np.float32)[None, :]
    cosine, sine = np.cos(angle), np.sin(angle)
    swap = np.zeros((DR, DR), np.float32)
    for i in range(half):
        swap[half + i, i] = -1.0
        swap[i, half + i] = 1.0
    trig = np.stack([np.concatenate([t, t], axis=1) for t in (cosine, sine)])
    return trig.astype(np.float32), swap


def for_rows(rows, step, body):
    def one(i, carry):
        body(pl.multiple_of(i * step, step))
        return carry

    lax.fori_loop(0, rows // step, one, 0)


def places():
    d, h = lax.axis_index("dp"), lax.axis_index("head")
    y, xh = d // 2, d % 2
    b, y0 = y // 2, y % 2
    a = (y0 + b) % 2
    z, r = h // 4, h % 4
    xl, c = r // 2, r % 2
    bits = {"A": a, "B": b, "X": xh}
    ya, yb, yab = y + 1 - 2 * y0, 3 - y, 2 - y + 2 * y0
    peer = {
        "A": (2 * ya + xh, h),
        "B": (2 * yb + xh, h),
        "X": (2 * y + 1 - xh, h),
        "AB": (2 * yab + xh, h),
        "AX": (2 * ya + 1 - xh, h),
        "BX": (2 * yb + 1 - xh, h),
        "ABX": (2 * yab + 1 - xh, h),
        "C": (d, h + 1 - 2 * c),
        "L": (d, h + 2 - 4 * xl),
    }
    for k in range(1, 8):
        peer["Z%d" % k] = (d, (h + 4 * k) % 32)
    return bits, peer, d, z, xl, c


def dot(left, right):
    return jnp.dot(left, right, preferred_element_type=F32)


def dot_nt(left, right):
    return lax.dot_general(left, right, (((1,), (1,)), ((), ())), preferred_element_type=F32)


def dot_tn(left, right):
    return lax.dot_general(left, right, (((0,), (0,)), ((), ())), preferred_element_type=F32)


def step_kernel(*refs):
    refs = list(refs)

    def take(n):
        out = refs[:n]
        del refs[:n]
        return out

    ql_hbm, kvl_hbm, dy_hbm, wq_hbm, wk_hbm, wv_hbm, trig_hbm, swap_hbm = take(8)
    g = take(G)
    s_out, lat_out = take(2)
    ql, kvlt, dy, wq, wk, wv, trig, swap, qlt, dqs, dkv = take(11)
    stg, rcv, ra, rb = take(N), take(N), take(N), take(N)
    lat, lrecv, lsum, zs, zr, lx, lxr, sq, sd, sl, slr, sc, scr, sf, sz = take(15)
    in_sem, rs_send, rs_recv, ag_send, ag_recv, l_send, l_recv, s_send, s_recv = take(9)

    loads = [
        pltpu.make_async_copy(src, dst, in_sem.at[i])
        for i, (src, dst) in enumerate((
            (kvl_hbm, kvlt), (wk_hbm, wk), (wv_hbm, wv), (ql_hbm, ql),
            (wq_hbm.at[:, pl.ds(0, QC)], wq.at[0]), (dy_hbm, dy), (trig_hbm, trig), (swap_hbm, swap),
            (wq_hbm.at[:, pl.ds(QC, QC)], wq.at[1]),
        ))
    ]
    for load in loads:
        load.start()
    bits, peer, d, z, xl, c = places()
    barrier = pltpu.get_barrier_semaphore()
    for where in peer.values():
        pl.semaphore_signal(barrier, inc=1, device_id=where, device_id_type=MESH)

    def remote(src, dst, send, recv, where):
        copy = pltpu.make_async_remote_copy(
            src_ref=src, dst_ref=dst, send_sem=send, recv_sem=recv,
            device_id=peer[where], device_id_type=MESH,
        )
        copy.start()
        return copy

    def cut(p):
        return PIECES[p][1], PIECES[p][3], STEPS[PIECES[p][1]]

    def product(p, lo, n):
        array, kind, r0, _ = PIECES[p]
        if kind == 2:
            return dot(kvlt[pl.ds(r0 + lo, n), :], dkv[array // 3])
        return dot(qlt[pl.ds(768 * kind + r0 + lo, n), :], dqs[array // 3])

    def area(p, s):
        rows = cut(p)[1]
        return (0, rows // 2, rows // 2 + rows // 4)[s], rows >> (s + 1)

    def dim(p, s):
        return ORDERS[cut(p)[0]][s]

    def rs_send_off(p, s):
        off, n = area(p, s)
        return remote(
            stg[p].at[pl.ds(off, n)], rcv[p].at[pl.ds(off, n)],
            rs_send.at[p, s], rs_recv.at[p, s], dim(p, s),
        )

    def rs_first(p):
        off, n = area(p, 0)
        away = pl.multiple_of((1 - bits[dim(p, 0)]) * n, 64)
        stg[p][:n, :] = product(p, away, n).astype(BF)
        return rs_send_off(p, 0)

    def rs_keep(p):
        off, n = area(p, 0)
        keep = pl.multiple_of(bits[dim(p, 0)] * n, 64)
        ra[p][...] = product(p, keep, n)

    def rs_second(p, copy):
        copy.wait()
        off, n = area(p, 1)
        bit = bits[dim(p, 1)]
        away, keep = (1 - bit) * n, bit * n
        rows = cut(p)[2]

        def total(lo):
            return ra[p][pl.ds(lo, rows), :] + rcv[p][pl.ds(lo, rows), :].astype(F32)

        def out(i):
            stg[p][pl.ds(off + i, rows), :] = total(pl.multiple_of(away + i, 16)).astype(BF)

        for_rows(n, rows, out)
        sent = rs_send_off(p, 1)

        def hold(i):
            rb[p][pl.ds(i, rows), :] = total(pl.multiple_of(keep + i, 16))

        for_rows(n, rows, hold)
        return sent

    def rs_third(p, copy):
        copy.wait()
        before, _ = area(p, 1)
        off, n = area(p, 2)
        away = (1 - bits[dim(p, 2)]) * n
        rows = cut(p)[2]

        def out(i):
            lo = pl.multiple_of(away + i, 16)
            stg[p][pl.ds(off + i, rows), :] = (
                rb[p][pl.ds(lo, rows), :]
                + rcv[p][pl.ds(pl.multiple_of(before + lo, 16), rows), :].astype(F32)
            ).astype(BF)

        for_rows(n, rows, out)
        return rs_send_off(p, 2)

    def owned(p, s):
        lo = PIECES[p][2]
        for t in range(s + 1):
            lo = lo + bits[dim(p, t)] * (cut(p)[1] >> (t + 1))
        return pl.multiple_of(lo, 16)

    def rs_last(p, copy):
        copy.wait()
        before, _ = area(p, 1)
        off, n = area(p, 2)
        keep = bits[dim(p, 2)] * n
        lo = owned(p, 2)
        rows = cut(p)[2]
        out = g[PIECES[p][0]]

        def body(i):
            at = pl.multiple_of(keep + i, 16)
            total = (
                rb[p][pl.ds(at, rows), :]
                + rcv[p][pl.ds(pl.multiple_of(before + at, 16), rows), :].astype(F32)
                + rcv[p][pl.ds(off + i, rows), :].astype(F32)
            )
            out[pl.ds(pl.multiple_of(lo + i, 16), rows), :] = total.astype(BF)
            square = total * total
            part = square[:, :128]
            for j in range(1, square.shape[1] // 128):
                part = part + square[:, 128 * j : 128 * (j + 1)]
            left = sq[...]
            for j in range(0, rows, 8):
                left = left + part[j : j + 8]
            sq[...] = left

        for_rows(n, rows, body)

    def ag_start(p, s):
        block = g[PIECES[p][0]].at[pl.ds(owned(p, s), cut(p)[1] >> (s + 1))]
        return remote(block, block, ag_send.at[p, s], ag_recv.at[p, s], dim(p, s))

    for load in loads[:3]:
        load.wait()
    plain = jnp.transpose(kvlt[:KL, :])
    key_rot = jnp.transpose(kvlt[KL:, :])
    scale = 1.0 / DQ**0.5
    allowed = lax.broadcasted_iota(jnp.int32, (ROWS, ROWS), 0) <= lax.broadcasted_iota(
        jnp.int32, (ROWS, ROWS), 1
    )
    rot = jnp.zeros((ROWS, DR), F32)
    moving = []
    for j in range(PAIRS):
        cols = slice(2 * DN * j, 2 * DN * (j + 1))
        keys = dot(plain, wk[:, cols]).astype(BF)
        values = dot(plain, wv[:, cols]).astype(BF)
        if j == 0:
            for load in loads[3:8]:
                load.wait()
            cosine, sine = trig[0], trig[1]
            turn = swap[...]
        else:
            loads[8].wait()
        queries = dot(ql[...], wq[j]).astype(BF)
        if j == 0:
            qlt[...] = jnp.transpose(ql[...])
        parts = []
        for n in range(2):
            q_plain = queries[:, DQ * n : DQ * n + DN]
            q_rot = queries[:, DQ * n + DN : DQ * (n + 1)]
            q_rope = (q_rot.astype(F32) * cosine + dot(q_rot, turn) * sine).astype(BF)
            key = keys[:, DN * n : DN * (n + 1)]
            value = values[:, DN * n : DN * (n + 1)]
            grad = dy[:, 2 * DN * j + DN * n : 2 * DN * j + DN * (n + 1)]
            q_all = jnp.concatenate([q_plain, q_rope], axis=1)
            k_all = jnp.concatenate([key, key_rot], axis=1)
            scores = jnp.where(allowed, dot_nt(k_all, q_all) * scale, -jnp.inf)
            top = jnp.max(scores, axis=0, keepdims=True)
            weights = jnp.exp(scores - top)
            probs = weights / jnp.sum(weights, axis=0, keepdims=True)
            dkv[j, :, 2 * DN + DN * n : 2 * DN + DN * (n + 1)] = dot(
                probs.astype(BF), grad
            ).astype(BF)
            dp = dot_nt(value, grad)
            mean = jnp.sum(dp * probs, axis=0, keepdims=True)
            ds = (probs * (dp - mean) * scale).astype(BF)
            dk = dot(ds, q_all)
            dkv[j, :, DN * n : DN * (n + 1)] = dk[:, :DN].astype(BF)
            rot = rot + dk[:, DN:].astype(BF).astype(F32)
            dq = dot_tn(ds, k_all)
            d_rope = dq[:, DN:].astype(BF)
            d_rot = d_rope.astype(F32) * cosine + dot_nt(d_rope, turn) * sine
            parts.append(jnp.concatenate([dq[:, :DN].astype(BF), d_rot.astype(BF)], axis=1))
        dqs[j] = jnp.concatenate(parts, axis=1)
        if j == 0:
            pl.semaphore_wait(barrier, len(peer))
        for p in range(N // PAIRS):
            moving.append(rs_first(N // PAIRS * j + p))

    lat[:, :, :, :QL] = (dot_nt(dqs[0], wq[0]) + dot_nt(dqs[1], wq[1])).reshape(16, 2, 8, QL)
    term = dot_nt(dkv[0, :, : 2 * DN], wk[:, : 2 * DN]) + dot_nt(dkv[1, :, : 2 * DN], wk[:, 2 * DN :])
    term = term + dot_nt(dkv[0, :, 2 * DN :], wv[:, : 2 * DN])
    term = term + dot_nt(dkv[1, :, 2 * DN :], wv[:, 2 * DN :])
    lat[:, :, :, QL : QL + KL] = term.reshape(16, 2, 8, KL)
    lat[:, :, :, QL + KL :] = jnp.concatenate([rot, jnp.zeros((ROWS, DR), F32)], axis=1).reshape(
        16, 2, 8, 128
    )
    core = remote(lat.at[:, 1 - c], lrecv, l_send.at[0], l_recv.at[0], "C")
    turns = [p + q for p in range(0, N, 3) for q in (0, 1, 2)]
    for p in turns:
        rs_keep(p)
    for p in turns[:3]:
        moving[p] = rs_second(p, moving[p])
    core.wait()

    def core_body(k, carry):
        lsum[k] = lat[k, c] + lrecv[k]
        return carry

    lax.fori_loop(0, 16, core_body, 0)

    def zs_body(k, carry):
        zs[k] = jnp.concatenate([lsum[2 * k], lsum[2 * k + 1]], axis=0).astype(BF)
        return carry

    lax.fori_loop(0, 8, zs_body, 0)
    zcopies = [
        remote(zs.at[(z + k) % 8], zr.at[k - 1], l_send.at[k], l_recv.at[k], "Z%d" % k)
        for k in range(1, 8)
    ]
    for p in turns[3:]:
        moving[p] = rs_second(p, moving[p])
    for p in turns:
        moving[p] = rs_third(p, moving[p])
    sq[...] = jnp.zeros((8, 128), F32)
    for p in turns:
        rs_last(p, moving[p])
        moving[p] = ag_start(p, 2)

    cube = [
        remote(sq, sd.at[d], s_send.at[i], s_recv.at[i], where)
        for i, where in enumerate(("A", "B", "X", "AB", "AX", "BX", "ABX"))
    ]
    sd[d] = sq[...]
    for copy in zcopies:
        copy.wait()
    lx[0] = lsum[2 * z]
    lx[1] = lsum[2 * z + 1]
    for k in range(7):
        got = zr[k].astype(F32)
        lx[0] = lx[0] + got[:8]
        lx[1] = lx[1] + got[8:]
    xcopy = remote(lx.at[1 - xl], lxr, l_send.at[8], l_recv.at[8], "L")
    for p in turns:
        moving[p].wait()
        moving[p] = ag_start(p, 1)
    for copy in cube:
        copy.wait()
    total = sd[0]
    for i in range(1, 8):
        total = total + sd[i]
    sl[...] = total
    ls = remote(sl, slr, s_send.at[7], s_recv.at[7], "L")
    for p in turns:
        moving[p].wait()
        moving[p] = ag_start(p, 0)
    ls.wait()
    sc[...] = sl[...] + slr[...]
    cs = remote(sc, scr, s_send.at[8], s_recv.at[8], "C")
    xcopy.wait()
    lat_out[...] = lx[xl] + lxr[...]
    cs.wait()
    sf[...] = sc[...] + scr[...]
    zsum = [
        remote(sf, sz.at[z], s_send.at[8 + k], s_recv.at[8 + k], "Z%d" % k) for k in range(1, 8)
    ]
    sz[z] = sf[...]
    for copy in zsum:
        copy.wait()
    s_out[...] = sz[...]
    for copy in moving:
        copy.wait()


def step(ql, kvl, dy, wq, wk, wv):
    trig, swap = tables()
    vmem = pl.BlockSpec(memory_space=pltpu.VMEM)
    hbm = pl.BlockSpec(memory_space=pltpu.HBM)

    def buffer(p, rows, dtype):
        return pltpu.VMEM((rows, SHAPES[PIECES[p][1]][1]), dtype)

    scratch = [
        pltpu.VMEM((ROWS, QL), BF),
        pltpu.VMEM((KL + DR, ROWS), BF),
        pltpu.VMEM((ROWS, HEADS * DN), BF),
        pltpu.VMEM((PAIRS, QL, QC), BF),
        pltpu.VMEM((KL, HEADS * DN), BF),
        pltpu.VMEM((KL, HEADS * DN), BF),
        pltpu.VMEM((2, ROWS, DR), F32),
        pltpu.VMEM((DR, DR), BF),
        pltpu.VMEM((QL, ROWS), BF),
        pltpu.VMEM((PAIRS, ROWS, QC), BF),
        pltpu.VMEM((PAIRS, ROWS, KC), BF),
    ]
    scratch += [buffer(p, PIECES[p][3] * 7 // 8, BF) for p in range(N)] * 2
    scratch += [buffer(p, PIECES[p][3] // 2, F32) for p in range(N)]
    scratch += [buffer(p, PIECES[p][3] // 4, F32) for p in range(N)]
    tile = (8, 128)
    scratch += [
        pltpu.VMEM((16, 2, 8, LAT), F32),
        pltpu.VMEM((16, 8, LAT), F32),
        pltpu.VMEM((16, 8, LAT), F32),
        pltpu.VMEM((8, 16, LAT), BF),
        pltpu.VMEM((7, 16, LAT), BF),
        pltpu.VMEM((2, 8, LAT), F32),
        pltpu.VMEM((8, LAT), F32),
        pltpu.VMEM(tile, F32),
        pltpu.VMEM((8,) + tile, F32),
    ]
    scratch += [pltpu.VMEM(tile, F32)] * 5 + [pltpu.VMEM((8,) + tile, F32)]
    dma = pltpu.SemaphoreType.DMA
    scratch += [dma((9,)), dma((N, 3)), dma((N, 3)), dma((N, 3)), dma((N, 3))]
    scratch += [dma((9,)), dma((9,)), dma((16,)), dma((16,))]
    args = (ql, kvl, dy, wq, wk, wv, jnp.asarray(trig), jnp.asarray(swap, BF))
    return pl.pallas_call(
        step_kernel,
        out_shape=tuple(jax.ShapeDtypeStruct(SHAPES[i % 3], BF) for i in range(G))
        + (jax.ShapeDtypeStruct((8, 8, 128), F32), jax.ShapeDtypeStruct((8, LAT), F32)),
        in_specs=[hbm] * 8,
        out_specs=(vmem,) * (G + 2),
        scratch_shapes=scratch,
        name="step",
        compiler_params=pltpu.CompilerParams(
            collective_id=0, has_side_effects=True, vmem_limit_bytes=46 << 20
        ),
    )(*(pltpu.with_memory_space_constraint(t, pltpu.HBM) for t in args))


def finish_kernel(count, *refs):
    s_ref, lat_ref = refs[:2]
    g = refs[2 : 2 + G]
    ql_out, kvl_out, q_out, k_out, v_out = refs[2 + G : 7 + G]
    buffers = refs[7 + G : 7 + 2 * G]
    kvl, sem = refs[7 + 2 * G :]
    kvl[...] = lat_ref[:, QL : QL + KL + DR]
    copies = []

    def start(src, dst):
        copy = pltpu.make_async_copy(src, dst, sem.at[len(copies)])
        copy.start()
        copies.append(copy)

    start(lat_ref.at[:, pl.ds(0, QL)], ql_out)
    start(kvl, kvl_out)
    total = jnp.sum(s_ref[...], axis=0)
    total = jnp.sum(total, axis=0, keepdims=True)
    total = jnp.sum(total, axis=1, keepdims=True)
    factor = jnp.minimum(1.0, max_rms * count**0.5 / jnp.sqrt(total + eps))
    for i in range(G):
        j, kind = i // 3, i % 3
        rows = SHAPES[kind][0] // SUB
        for u in range(SUB):
            at = pl.ds(rows * u, rows)

            def body(lo):
                where = pl.ds(pl.multiple_of(rows * u + lo, 16), 64)
                buffers[i][where, :] = (g[i][where, :].astype(F32) * factor).astype(BF)

            for_rows(rows, 64, body)
            if kind == 2:
                half = pl.ds(2 * DN * j, 2 * DN)
                start(buffers[i].at[at, pl.ds(0, 2 * DN)], k_out.at[at, half])
                start(buffers[i].at[at, pl.ds(2 * DN, 2 * DN)], v_out.at[at, half])
            else:
                start(
                    buffers[i].at[at],
                    q_out.at[pl.ds(768 * kind + rows * u, rows), pl.ds(QC * j, QC)],
                )
    for copy in copies:
        copy.wait()


def finish(count, s, lat, pieces):
    vmem = pl.BlockSpec(memory_space=pltpu.VMEM)
    hbm = pl.BlockSpec(memory_space=pl.ANY)
    return pl.pallas_call(
        functools.partial(finish_kernel, count),
        out_shape=(
            jax.ShapeDtypeStruct((8, QL), F32),
            jax.ShapeDtypeStruct((8, KL + DR), F32),
            jax.ShapeDtypeStruct((QL, HEADS * DQ), BF),
            jax.ShapeDtypeStruct((KL, HEADS * DN), BF),
            jax.ShapeDtypeStruct((KL, HEADS * DN), BF),
        ),
        in_specs=[vmem] * (G + 2),
        out_specs=(hbm,) * 5,
        scratch_shapes=[pltpu.VMEM(SHAPES[i % 3], BF) for i in range(G)]
        + [pltpu.VMEM((8, KL + DR), F32), pltpu.SemaphoreType.DMA((2 + SUB * PAIRS * 4,))],
        name="finish",
        compiler_params=pltpu.CompilerParams(vmem_limit_bytes=16 << 20),
    )(s, lat, *pieces)


def per_device(query_latent, kv_latent, out_grad, query_up, key_up, value_up):
    width = lax.axis_size("head")
    count = (QL * query_up.shape[1] + 2 * KL * key_up.shape[1]) * width
    *pieces, s, lat = step(query_latent, kv_latent.T, out_grad, query_up, key_up, value_up)
    return tuple(finish(count, s, lat, pieces))


def solution(mesh):
    placed = (
        P("dp", None),
        P("dp", None),
        P("dp", "head"),
        P(None, "head"),
        P(None, "head"),
        P(None, "head"),
    )
    return jax.shard_map(
        per_device,
        mesh=mesh,
        in_specs=placed,
        out_specs=(
            P(("dp", "head"), None),
            P(("dp", "head"), None),
            P(None, "head"),
            P(None, "head"),
            P(None, "head"),
        ),
        check_vma=False,
    )
```

time: 68.6 us -> 61.4 us (0.90)
  Pallas kernels: 67.8 us -> 60.7 us
    pallas_call x1, Pallas kernels: 65.5 us -> 58.6 us  [step(): pl.pallas_call(step_kernel, out_shape=tuple((jax.ShapeDtypeStruct(SHAPES[...]
where the time goes in v3:
time: 61.4 us; the launch traced here: 61.3 us
  Pallas kernels  60.7 us (99%)
  between operations  0.64 us (1%)
    pallas_call x1, Pallas kernels, step(): pl.pallas_call(step_kernel, out_shape=tuple((jax.ShapeDtypeStruct(SHAPES[...  58.6 us
    pallas_call x1, Pallas kernels, finish(): pl.pallas_call(functools.partial(finish_kernel, count), out_shape=(jax.Sh...  2.08 us

profile of v3, /device:TPU:2, one launch (start us, length us, event | category | flops | bytes accessed | tf_op | source)
XLA Modules:
  0.0 61.3 jit_solution(13127283289284959625)
XLA Ops:
  0.6 58.6 %step.1 = (bf16[768,384]{1,0:T(8,128)(2,1)S(1)}, bf16[768,384]{1,0:T(8,128)(2,1)S(1)}, bf16[512,512]{1,0:T(8,128)(2,1)S(1)}, bf16[768,384]{1,0:T(8,128)(2,1)S(1)...) custom-call(bf16[256,1536]{1,0:T(8,128)(2,1)} %refs_0_.1, ...), custom_call_target="tpu_custom_call" | custom-call | tf_op jit(solution)/shard_map/step/pallas_call | solution.py:435
  59.3 2.1 %finish.1 = (f32[8,1536]{1,0:T(8,128)}, f32[8,576]{1,0:T(8,128)}, bf16[1536,768]{1,0:T(8,128)(2,1)}, bf16[512,512]{1,0:T(8,128)(2,1)}, bf16[512,512]{1,0:T(8,128)(2,1)}) custom-call(f32[8,8,128]{2,1,0:T(8,128)S(1)} %get-tuple-element.13.refs_0_, f32[8,2176]{1,0:T(8,128)S(1)} %get-tuple-element.14.refs_1_, bf16[768,384]{1,0:T(8,128)(2,1)S(1)} %get-tuple-element.15.refs_2_, ...), custom_call_target="tpu_custom_call" | custom-call | tf_op jit(solution)/shard_map/finish/pallas_call | solution.py:496

commit v4 on v3

v4 whole, which is shorter than its diff:
```python
import functools

import jax
import jax.numpy as jnp
import numpy as np
from jax import lax
from jax.experimental import pallas as pl
from jax.experimental.pallas import tpu as pltpu
from jax.sharding import PartitionSpec as P

QL = 1536
KL = 512
DN = 128
DR = 64
DQ = DN + DR
ROWS = 256
HEADS = 4
LAT = 2176

max_rms = 1.0
eps = 1e-06

MESH = pl.DeviceIdType.MESH
BF = jnp.bfloat16
F32 = jnp.float32

PAIRS = 2
QC = 2 * DQ
KC = 4 * DN
TURNS = ("XBA", "AXB", "BAX")
QUERY = tuple(
    (768 * c + 256 * u, 256, QC, ("AB", "BA")[c], TURNS[u]) for u in range(3) for c in range(2)
)
KEYVAL = tuple(
    (j, 256 * u, 256, KC, ("ABX", "BAX")[u], ("BAX", "ABX")[u]) for j in range(PAIRS) for u in range(2)
)
NQ, NK = len(QUERY), len(KEYVAL)
PIECES = QUERY + tuple(k[1:] for k in KEYVAL)
N = NQ + NK
STEP = 32


def tables():
    half = DR // 2
    freqs = np.float32(10000.0) ** (np.float32(-2.0) * np.arange(half, dtype=np.float32) / DR)
    angle = np.arange(ROWS, dtype=np.float32)[:, None] * freqs.astype(np.float32)[None, :]
    cosine, sine = np.cos(angle), np.sin(angle)
    swap = np.zeros((DR, DR), np.float32)
    for i in range(half):
        swap[half + i, i] = -1.0
        swap[i, half + i] = 1.0
    trig = np.concatenate([cosine, cosine, sine, sine], axis=1)
    return trig.astype(np.float32), swap


def for_rows(rows, step, body):
    def one(i, carry):
        body(pl.multiple_of(i * step, step))
        return carry

    lax.fori_loop(0, rows // step, one, 0)


def places():
    d, h = lax.axis_index("dp"), lax.axis_index("head")
    y, xh = d // 2, d % 2
    b, y0 = y // 2, y % 2
    a = (y0 + b) % 2
    z, r = h // 4, h % 4
    xl, c = r // 2, r % 2
    bits = {"A": a, "B": b, "X": xh}
    ya, yb, yab = y + 1 - 2 * y0, 3 - y, 2 - y + 2 * y0
    peer = {
        "A": (2 * ya + xh, h),
        "B": (2 * yb + xh, h),
        "X": (2 * y + 1 - xh, h),
        "AB": (2 * yab + xh, h),
        "AX": (2 * ya + 1 - xh, h),
        "BX": (2 * yb + 1 - xh, h),
        "ABX": (2 * yab + 1 - xh, h),
        "C": (d, h + 1 - 2 * c),
        "L": (d, h + 2 - 4 * xl),
    }
    for k in range(1, 8):
        peer["Z%d" % k] = (d, (h + 4 * k) % 32)
    return bits, peer, d, z, xl, c


def dot(left, right):
    return jnp.dot(left, right, preferred_element_type=F32)


def dot_nt(left, right):
    return lax.dot_general(left, right, (((1,), (1,)), ((), ())), preferred_element_type=F32)


def dot_tn(left, right):
    return lax.dot_general(left, right, (((0,), (0,)), ((), ())), preferred_element_type=F32)


def step_kernel(*refs):
    refs = list(refs)

    def take(n):
        out = refs[:n]
        del refs[:n]
        return out

    ql_hbm, kvl_hbm, dy_hbm, wq_hbm, wk_hbm, wv_hbm, trig_hbm, swap_hbm = take(8)
    g = take(N)
    s_out, lat_out = take(2)
    ql, kvlt, dy, wq, wk, wv, trig, swap, qx, qlt, dq_away, dqs, dkv = take(13)
    stg, rcv, ra, rb = take(N), take(N), take(N), take(N)
    lat, lrecv, lsum, zs, zr, lx, lxr, sq, sd, sl, slr, sc, scr, sf, sz = take(15)
    in_sem, rs_send, rs_recv, ag_send, ag_recv, q_send, q_recv, l_send, l_recv, s_send, s_recv = take(11)

    def pair(ref, j, width):
        return ref.at[:, pl.ds(width * j, width)]

    loads = [
        pltpu.make_async_copy(src, dst, in_sem.at[i])
        for i, (src, dst) in enumerate((
            (kvl_hbm, kvlt), (pair(wk_hbm, 0, 2 * DN), wk.at[0]), (pair(wk_hbm, 1, 2 * DN), wk.at[1]),
            (pair(wv_hbm, 0, 2 * DN), wv.at[0]), (pair(wv_hbm, 1, 2 * DN), wv.at[1]), (ql_hbm, ql),
            (trig_hbm, trig), (swap_hbm, swap), (pair(wq_hbm, 0, QC), wq.at[0]),
            (pair(wq_hbm, 1, QC), wq.at[1]), (pair(dy_hbm, 0, 2 * DN), dy.at[0]),
            (pair(dy_hbm, 1, 2 * DN), dy.at[1]),
        ))
    ]
    for load in loads:
        load.start()
    bits, peer, d, z, xl, c = places()
    barrier = pltpu.get_barrier_semaphore()
    for where in peer.values():
        pl.semaphore_signal(barrier, inc=1, device_id=where, device_id_type=MESH)

    def remote(src, dst, send, recv, where):
        copy = pltpu.make_async_remote_copy(
            src_ref=src, dst_ref=dst, send_sem=send, recv_sem=recv,
            device_id=peer[where], device_id_type=MESH,
        )
        copy.start()
        return copy

    def product(p, lo, n):
        r0 = PIECES[p][0]
        if p >= NQ:
            return dot(kvlt[pl.ds(r0 + lo, n), :], dkv[KEYVAL[p - NQ][0]])
        return dot(qlt[pl.ds(r0 + lo, n), :], dqs[...])

    def area(p, s):
        rows = PIECES[p][1]
        return (0, rows // 2, rows // 2 + rows // 4)[s], rows >> (s + 1)

    def bit(p, s):
        return bits[PIECES[p][3][s]]

    def rs_send_off(p, s):
        off, n = area(p, s)
        return remote(
            stg[p].at[pl.ds(off, n)], rcv[p].at[pl.ds(off, n)],
            rs_send.at[p, s], rs_recv.at[p, s], PIECES[p][3][s],
        )

    def rs_first(p):
        off, n = area(p, 0)
        away = pl.multiple_of((1 - bit(p, 0)) * n, 128)
        stg[p][:n, :] = product(p, away, n).astype(BF)
        return rs_send_off(p, 0)

    def rs_keep(p):
        off, n = area(p, 0)
        keep = pl.multiple_of(bit(p, 0) * n, 128)
        ra[p][...] = product(p, keep, n)

    def rs_second(p, copy):
        copy.wait()
        off, n = area(p, 1)
        away, keep = (1 - bit(p, 1)) * n, bit(p, 1) * n

        def total(lo):
            return ra[p][pl.ds(lo, STEP), :] + rcv[p][pl.ds(lo, STEP), :].astype(F32)

        def out(i):
            stg[p][pl.ds(off + i, STEP), :] = total(pl.multiple_of(away + i, 32)).astype(BF)

        for_rows(n, STEP, out)
        sent = rs_send_off(p, 1)

        def hold(i):
            rb[p][pl.ds(i, STEP), :] = total(pl.multiple_of(keep + i, 32))

        for_rows(n, STEP, hold)
        return sent

    def rs_third(p, copy):
        copy.wait()
        before, _ = area(p, 1)
        off, n = area(p, 2)
        away = (1 - bit(p, 2)) * n

        def out(i):
            lo = pl.multiple_of(away + i, 32)
            stg[p][pl.ds(off + i, STEP), :] = (
                rb[p][pl.ds(lo, STEP), :]
                + rcv[p][pl.ds(pl.multiple_of(before + lo, 32), STEP), :].astype(F32)
            ).astype(BF)

        for_rows(n, STEP, out)
        return rs_send_off(p, 2)

    def rs_last(p, copy):
        copy.wait()
        before, n = area(p, 1)
        if p >= NQ:
            off, n = area(p, 2)
            keep = bit(p, 2) * n
            place = (bit(p, 0), bit(p, 1), bit(p, 2))
        else:
            keep = 0
            place = (bits["X"], bit(p, 0), bit(p, 1))

        def body(i):
            at = pl.multiple_of(keep + i, 32)
            total = rb[p][pl.ds(at, STEP), :] + rcv[p][
                pl.ds(pl.multiple_of(before + at, 32), STEP), :
            ].astype(F32)
            if p >= NQ:
                total = total + rcv[p][pl.ds(off + i, STEP), :].astype(F32)
            g[p][place + (pl.ds(i, STEP), slice(None))] = total.astype(BF)
            square = total * total
            part = square[:, :128]
            for j in range(1, square.shape[1] // 128):
                part = part + square[:, 128 * j : 128 * (j + 1)]
            sq[...] = sq[...] + part[:8] + part[8:16] + part[16:24] + part[24:32]

        for_rows(n, STEP, body)

    def ag_start(p, s):
        order = PIECES[p][4]
        dims = PIECES[p][3] if p >= NQ else "X" + PIECES[p][3]
        where = tuple(
            pl.ds(0, 2) if name in order[:s] else pl.ds(bits[name], 1) for name in dims
        )
        block = g[p].at[where]
        return remote(block, block, ag_send.at[p, s], ag_recv.at[p, s], order[s])

    for load in loads[:5]:
        load.wait()
    plain = jnp.transpose(kvlt[:KL, :])
    key_rot = jnp.transpose(kvlt[KL:, :])
    scale = 1.0 / DQ**0.5
    allowed = lax.broadcasted_iota(jnp.int32, (ROWS, ROWS), 0) <= lax.broadcasted_iota(
        jnp.int32, (ROWS, ROWS), 1
    )
    rot = jnp.zeros((ROWS, DR), F32)
    loads[5].wait()
    pl.semaphore_wait(barrier, len(peer))
    half = pl.ds(pl.multiple_of(c * (QL // 2), 128), QL // 2)
    q_copy = remote(ql.at[:, half], qx.at[:, half], q_send.at[0], q_recv.at[0], "X")
    qlt[:, :ROWS] = jnp.transpose(ql[...])
    for load in loads[6:]:
        load.wait()
    cosine, sine = trig[:, :DR], trig[:, DR:]
    turn = swap[...]
    for t in range(PAIRS):
        j = bits["X"] if t else 1 - bits["X"]
        keys = dot(plain, wk[j]).astype(BF)
        values = dot(plain, wv[j]).astype(BF)
        queries = dot(ql[...], wq[j]).astype(BF)
        parts = []
        for n in range(2):
            q_plain = queries[:, DQ * n : DQ * n + DN]
            q_rot = queries[:, DQ * n + DN : DQ * (n + 1)]
            q_rope = (q_rot.astype(F32) * cosine + dot(q_rot, turn) * sine).astype(BF)
            key = keys[:, DN * n : DN * (n + 1)]
            value = values[:, DN * n : DN * (n + 1)]
            grad = dy[j, :, DN * n : DN * (n + 1)]
            q_all = jnp.concatenate([q_plain, q_rope], axis=1)
            k_all = jnp.concatenate([key, key_rot], axis=1)
            scores = jnp.where(allowed, dot_nt(k_all, q_all) * scale, -jnp.inf)
            top = jnp.max(scores, axis=0, keepdims=True)
            weights = jnp.exp(scores - top)
            probs = weights / jnp.sum(weights, axis=0, keepdims=True)
            dkv[j, :, 2 * DN + DN * n : 2 * DN + DN * (n + 1)] = dot(
                probs.astype(BF), grad
            ).astype(BF)
            dp = dot_nt(value, grad)
            mean = jnp.sum(dp * probs, axis=0, keepdims=True)
            ds = (probs * (dp - mean) * scale).astype(BF)
            dk = dot(ds, q_all)
            dkv[j, :, DN * n : DN * (n + 1)] = dk[:, :DN].astype(BF)
            rot = rot + dk[:, DN:].astype(BF).astype(F32)
            dq = dot_tn(ds, k_all)
            d_rope = dq[:, DN:].astype(BF)
            d_rot = d_rope.astype(F32) * cosine + dot_nt(d_rope, turn) * sine
            parts.append(jnp.concatenate([dq[:, :DN].astype(BF), d_rot.astype(BF)], axis=1))
        if t == 0:
            dq_away[...] = jnp.concatenate(parts, axis=1)
            d_copy = remote(
                dq_away, dqs.at[pl.ds(ROWS, ROWS)], q_send.at[1], q_recv.at[1], "X"
            )
        else:
            dqs[:ROWS, :] = jnp.concatenate(parts, axis=1)
    keyval = range(NQ, N)
    moving = [None] * N
    for p in keyval:
        moving[p] = rs_first(p)

    own = bits["X"]
    lat[:, :, :, :QL] = (dot_nt(dq_away[...], wq[1 - own]) + dot_nt(dqs[:ROWS, :], wq[own])).reshape(
        16, 2, 8, QL
    )
    term = dot_nt(dkv[0, :, : 2 * DN], wk[0]) + dot_nt(dkv[1, :, : 2 * DN], wk[1])
    term = term + dot_nt(dkv[0, :, 2 * DN :], wv[0]) + dot_nt(dkv[1, :, 2 * DN :], wv[1])
    lat[:, :, :, QL : QL + KL] = term.reshape(16, 2, 8, KL)
    lat[:, :, :, QL + KL :] = jnp.concatenate([rot, jnp.zeros((ROWS, DR), F32)], axis=1).reshape(
        16, 2, 8, 128
    )
    core = remote(lat.at[:, 1 - c], lrecv, l_send.at[0], l_recv.at[0], "C")
    for p in keyval:
        rs_keep(p)
    q_copy.wait()
    forward = remote(qx.at[:, half], qx.at[:, half], q_send.at[2], q_recv.at[2], "C")
    core.wait()

    def core_body(k, carry):
        lsum[k] = lat[k, c] + lrecv[k]
        return carry

    lax.fori_loop(0, 16, core_body, 0)

    def zs_body(k, carry):
        zs[k] = jnp.concatenate([lsum[2 * k], lsum[2 * k + 1]], axis=0).astype(BF)
        return carry

    lax.fori_loop(0, 8, zs_body, 0)
    zcopies = [
        remote(zs.at[(z + k) % 8], zr.at[k - 1], l_send.at[k], l_recv.at[k], "Z%d" % k)
        for k in range(1, 8)
    ]
    forward.wait()
    qlt[:, ROWS:] = jnp.transpose(qx[...])
    for p in keyval[:2]:
        moving[p] = rs_second(p, moving[p])
    d_copy.wait()
    for p in range(NQ):
        moving[p] = rs_first(p)
    for p in keyval[2:]:
        moving[p] = rs_second(p, moving[p])
    for p in range(NQ):
        rs_keep(p)
    for p in keyval:
        moving[p] = rs_third(p, moving[p])
    sq[...] = jnp.zeros((8, 128), F32)
    for p in keyval:
        rs_last(p, moving[p])
        moving[p] = ag_start(p, 0)
    for p in range(NQ):
        moving[p] = rs_second(p, moving[p])
    for p in keyval:
        moving[p].wait()
        moving[p] = ag_start(p, 1)
    for p in range(NQ):
        rs_last(p, moving[p])
        moving[p] = ag_start(p, 0)

    cube = [
        remote(sq, sd.at[d], s_send.at[i], s_recv.at[i], where)
        for i, where in enumerate(("A", "B", "X", "AB", "AX", "BX", "ABX"))
    ]
    sd[d] = sq[...]
    for p in keyval:
        moving[p].wait()
        moving[p] = ag_start(p, 2)
    for p in range(NQ):
        moving[p].wait()
        moving[p] = ag_start(p, 1)
    for copy in cube:
        copy.wait()
    total = sd[0]
    for i in range(1, 8):
        total = total + sd[i]
    sl[...] = total
    ls = remote(sl, slr, s_send.at[7], s_recv.at[7], "L")
    for copy in zcopies:
        copy.wait()
    lx[0] = lsum[2 * z]
    lx[1] = lsum[2 * z + 1]
    for k in range(7):
        got = zr[k].astype(F32)
        lx[0] = lx[0] + got[:8]
        lx[1] = lx[1] + got[8:]
    xcopy = remote(lx.at[1 - xl], lxr, l_send.at[8], l_recv.at[8], "L")
    for p in range(NQ):
        moving[p].wait()
        moving[p] = ag_start(p, 2)
    ls.wait()
    sc[...] = sl[...] + slr[...]
    cs = remote(sc, scr, s_send.at[8], s_recv.at[8], "C")
    xcopy.wait()
    lat_out[...] = lx[xl] + lxr[...]
    cs.wait()
    sf[...] = sc[...] + scr[...]
    zsum = [
        remote(sf, sz.at[z], s_send.at[8 + k], s_recv.at[8 + k], "Z%d" % k) for k in range(1, 8)
    ]
    sz[z] = sf[...]
    for copy in zsum:
        copy.wait()
    s_out[...] = sz[...]
    for copy in moving:
        copy.wait()


def gathered(p):
    return (2, 2, 2, PIECES[p][1] // (8 if p >= NQ else 4), PIECES[p][2])


def step(ql, kvl, dy, wq, wk, wv):
    trig, swap = tables()
    vmem = pl.BlockSpec(memory_space=pltpu.VMEM)
    hbm = pl.BlockSpec(memory_space=pltpu.HBM)

    def buffer(p, part, dtype):
        return pltpu.VMEM((PIECES[p][1] * part // 8, PIECES[p][2]), dtype)

    scratch = [
        pltpu.VMEM((ROWS, QL), BF),
        pltpu.VMEM((KL + DR, ROWS), BF),
        pltpu.VMEM((PAIRS, ROWS, 2 * DN), BF),
        pltpu.VMEM((PAIRS, QL, QC), BF),
        pltpu.VMEM((PAIRS, KL, 2 * DN), BF),
        pltpu.VMEM((PAIRS, KL, 2 * DN), BF),
        pltpu.VMEM((ROWS, 2 * DR), F32),
        pltpu.VMEM((DR, DR), BF),
        pltpu.VMEM((ROWS, QL), BF),
        pltpu.VMEM((QL, 2 * ROWS), BF),
        pltpu.VMEM((ROWS, QC), BF),
        pltpu.VMEM((2 * ROWS, QC), BF),
        pltpu.VMEM((PAIRS, ROWS, KC), BF),
    ]
    scratch += [buffer(p, 7 if p >= NQ else 6, BF) for p in range(N)] * 2
    scratch += [buffer(p, 4, F32) for p in range(N)]
    scratch += [buffer(p, 2, F32) for p in range(N)]
    tile = (8, 128)
    scratch += [
        pltpu.VMEM((16, 2, 8, LAT), F32),
        pltpu.VMEM((16, 8, LAT), F32),
        pltpu.VMEM((16, 8, LAT), F32),
        pltpu.VMEM((8, 16, LAT), BF),
        pltpu.VMEM((7, 16, LAT), BF),
        pltpu.VMEM((2, 8, LAT), F32),
        pltpu.VMEM((8, LAT), F32),
        pltpu.VMEM(tile, F32),
        pltpu.VMEM((8,) + tile, F32),
    ]
    scratch += [pltpu.VMEM(tile, F32)] * 5 + [pltpu.VMEM((8,) + tile, F32)]
    dma = pltpu.SemaphoreType.DMA
    scratch += [dma((12,)), dma((N, 3)), dma((N, 3)), dma((N, 3)), dma((N, 3))]
    scratch += [dma((3,)), dma((3,)), dma((9,)), dma((9,)), dma((16,)), dma((16,))]
    args = (ql, kvl, dy, wq, wk, wv, jnp.asarray(trig), jnp.asarray(swap, BF))
    return pl.pallas_call(
        step_kernel,
        out_shape=tuple(jax.ShapeDtypeStruct(gathered(p), BF) for p in range(N))
        + (jax.ShapeDtypeStruct((8, 8, 128), F32), jax.ShapeDtypeStruct((8, LAT), F32)),
        in_specs=[hbm] * 8,
        out_specs=(vmem,) * (N + 2),
        scratch_shapes=scratch,
        name="step",
        compiler_params=pltpu.CompilerParams(
            collective_id=0, has_side_effects=True, vmem_limit_bytes=46 << 20
        ),
    )(*(pltpu.with_memory_space_constraint(t, pltpu.HBM) for t in args))


def finish_kernel(count, *refs):
    s_ref, lat_ref = refs[:2]
    g = refs[2 : 2 + N]
    ql_out, kvl_out, q_out, k_out, v_out = refs[2 + N : 7 + N]
    buffers = refs[7 + N : 7 + 2 * N]
    kvl, sem = refs[7 + 2 * N :]
    kvl[...] = lat_ref[:, QL : QL + KL + DR]
    copies = []

    def start(src, dst):
        copy = pltpu.make_async_copy(src, dst, sem.at[len(copies)])
        copy.start()
        copies.append(copy)

    start(lat_ref.at[:, pl.ds(0, QL)], ql_out)
    start(kvl, kvl_out)
    total = jnp.sum(s_ref[...], axis=0)
    total = jnp.sum(total, axis=0, keepdims=True)
    total = jnp.sum(total, axis=1, keepdims=True)
    factor = jnp.minimum(1.0, max_rms * count**0.5 / jnp.sqrt(total + eps))
    for p in range(N):
        r0, rows = PIECES[p][:2]
        for a in range(2):

            def body(i, carry):
                one, two = i // 2, i % 2
                buffers[p][a, one, two] = (g[p][a, one, two].astype(F32) * factor).astype(BF)
                return carry

            lax.fori_loop(0, 4, body, 0)
            if p < NQ:
                for one in range(2):
                    for two in range(2):
                        n = rows // 4
                        start(
                            buffers[p].at[a, one, two],
                            q_out.at[pl.ds(r0 + n * (2 * one + two), n), pl.ds(QC * a, QC)],
                        )
            else:
                pair = KEYVAL[p - NQ][0]
                half = pl.ds(2 * DN * pair, 2 * DN)
                n = rows // 8
                for one in range(2):
                    for two in range(2):
                        at = pl.ds(r0 + n * (4 * a + 2 * one + two), n)
                        block = buffers[p].at[a, one, two]
                        start(block.at[:, pl.ds(0, 2 * DN)], k_out.at[at, half])
                        start(block.at[:, pl.ds(2 * DN, 2 * DN)], v_out.at[at, half])
    for copy in copies:
        copy.wait()


def finish(count, s, lat, pieces):
    vmem = pl.BlockSpec(memory_space=pltpu.VMEM)
    hbm = pl.BlockSpec(memory_space=pl.ANY)
    return pl.pallas_call(
        functools.partial(finish_kernel, count),
        out_shape=(
            jax.ShapeDtypeStruct((8, QL), F32),
            jax.ShapeDtypeStruct((8, KL + DR), F32),
            jax.ShapeDtypeStruct((QL, HEADS * DQ), BF),
            jax.ShapeDtypeStruct((KL, HEADS * DN), BF),
            jax.ShapeDtypeStruct((KL, HEADS * DN), BF),
        ),
        in_specs=[vmem] * (N + 2),
        out_specs=(hbm,) * 5,
        scratch_shapes=[pltpu.VMEM(gathered(p), BF) for p in range(N)]
        + [pltpu.VMEM((8, KL + DR), F32), pltpu.SemaphoreType.DMA((2 + 8 * NQ + 16 * NK,))],
        name="finish",
        compiler_params=pltpu.CompilerParams(vmem_limit_bytes=16 << 20),
    )(s, lat, *pieces)


def per_device(query_latent, kv_latent, out_grad, query_up, key_up, value_up):
    width = lax.axis_size("head")
    count = (QL * query_up.shape[1] + 2 * KL * key_up.shape[1]) * width
    *pieces, s, lat = step(query_latent, kv_latent.T, out_grad, query_up, key_up, value_up)
    return tuple(finish(count, s, lat, pieces))


def solution(mesh):
    placed = (
        P("dp", None),
        P("dp", None),
        P("dp", "head"),
        P(None, "head"),
        P(None, "head"),
        P(None, "head"),
    )
    return jax.shard_map(
        per_device,
        mesh=mesh,
        in_specs=placed,
        out_specs=(
            P(("dp", "head"), None),
            P(("dp", "head"), None),
            P(None, "head"),
            P(None, "head"),
            P(None, "head"),
        ),
        check_vma=False,
    )
```

time: 61.4 us -> 77.4 us (1.26); the launches traced: 61.3 us -> 76.2 us
  Pallas kernels: 60.7 us -> 75.5 us
    pallas_call x1, Pallas kernels: 58.6 us -> 72.2 us  [step(): pl.pallas_call(step_kernel, out_shape=tuple((jax.ShapeDtypeStruct(gathere...]
    pallas_call x1, Pallas kernels: 2.08 us -> 3.32 us  [finish(): pl.pallas_call(functools.partial(finish_kernel, count), out_shape=(jax.Sh...]
where the time goes in v4:
time: 77.4 us; the launch traced here: 76.2 us
  Pallas kernels  75.5 us (98%)
    pallas_call x1, Pallas kernels, step(): pl.pallas_call(step_kernel, out_shape=tuple((jax.ShapeDtypeStruct(gathere...  72.2 us
    pallas_call x1, Pallas kernels, finish(): pl.pallas_call(functools.partial(finish_kernel, count), out_shape=(jax.Sh...  3.32 us

profile of v4, /device:TPU:2, one launch (start us, length us, event | category | flops | bytes accessed | tf_op | source)
XLA Modules:
  0.0 76.2 jit_solution(2476923854097219256)
XLA Ops:
  0.6 72.2 %step.1 = (bf16[2,2,2,64,384]{4,3,2,1,0:T(8,128)(2,1)S(1)}, bf16[2,2,2,64,384]{4,3,2,1,0:T(8,128)(2,1)S(1)}, bf16[2,2,2,64,384]{4,3,2,1,0:T(8,128)(2,1)S(1)}, bf...) custom-call(bf16[256,1536]{1,0:T(8,128)(2,1)} %refs_0_.1, ...), custom_call_target="tpu_custom_call" | custom-call | tf_op jit(solution)/shard_map/step/pallas_call | solution.py:463
  72.8 3.3 %finish.1 = (f32[8,1536]{1,0:T(8,128)}, f32[8,576]{1,0:T(8,128)}, bf16[1536,768]{1,0:T(8,128)(2,1)}, bf16[512,512]{1,0:T(8,128)(2,1)}, bf16[512,512]{1,0:T(8,128)(2,1)}) custom-call(f32[8,8,128]{2,1,0:T(8,128)S(1)} %get-tuple-element.17.refs_0_, f32[8,2176]{1,0:T(8,128)S(1)} %get-tuple-element.18.refs_1_, ...), custom_call_target="tpu_custom_call" | custom-call | tf_op jit(solution)/shard_map/finish/pallas_call | solution.py:532

commit v5 on v3

--- a/solution.py
+++ b/solution.py
@@ -30,14 +30,16 @@
 SHAPES = ((768, QC), (768, QC), (512, KC))
 G = PAIRS * len(SHAPES)
 ORDERS = ("ABX", "BXA", "XAB")
-SUB = 2
+SUBS = (2, 2, 2)
 PIECES = tuple(
-    (3 * j + kind, kind, SHAPES[kind][0] // SUB * u, SHAPES[kind][0] // SUB)
+    (3 * j + kind, kind, SHAPES[kind][0] // SUBS[kind] * u, SHAPES[kind][0] // SUBS[kind])
     for j in range(PAIRS)
-    for u in range(SUB)
+    for u in range(max(SUBS))
     for kind in range(3)
+    if u < SUBS[kind]
 )
 N = len(PIECES)
+CUTS = 2
 STEPS = (48, 48, 32)
 
 
@@ -315,7 +317,7 @@
         16, 2, 8, 128
     )
     core = remote(lat.at[:, 1 - c], lrecv, l_send.at[0], l_recv.at[0], "C")
-    turns = [p + q for p in range(0, N, 3) for q in (0, 1, 2)]
+    turns = list(range(N))
     for p in turns:
         rs_keep(p)
     for p in turns[:3]:
@@ -351,6 +353,16 @@
         for i, where in enumerate(("A", "B", "X", "AB", "AX", "BX", "ABX"))
     ]
     sd[d] = sq[...]
+    for p in turns:
+        moving[p].wait()
+        moving[p] = ag_start(p, 1)
+    for copy in cube:
+        copy.wait()
+    total = sd[0]
+    for i in range(1, 8):
+        total = total + sd[i]
+    sl[...] = total
+    ls = remote(sl, slr, s_send.at[7], s_recv.at[7], "L")
     for copy in zcopies:
         copy.wait()
     lx[0] = lsum[2 * z]
@@ -360,16 +372,6 @@
         lx[0] = lx[0] + got[:8]
         lx[1] = lx[1] + got[8:]
     xcopy = remote(lx.at[1 - xl], lxr, l_send.at[8], l_recv.at[8], "L")
-    for p in turns:
-        moving[p].wait()
-        moving[p] = ag_start(p, 1)
-    for copy in cube:
-        copy.wait()
-    total = sd[0]
-    for i in range(1, 8):
-        total = total + sd[i]
-    sl[...] = total
-    ls = remote(sl, slr, s_send.at[7], s_recv.at[7], "L")
     for p in turns:
         moving[p].wait()
         moving[p] = ag_start(p, 0)
@@ -468,15 +470,14 @@
     factor = jnp.minimum(1.0, max_rms * count**0.5 / jnp.sqrt(total + eps))
     for i in range(G):
         j, kind = i // 3, i % 3
-        rows = SHAPES[kind][0] // SUB
-        for u in range(SUB):
+        rows = SHAPES[kind][0] // CUTS
+        for u in range(CUTS):
             at = pl.ds(rows * u, rows)
 
-            def body(lo):
-                where = pl.ds(pl.multiple_of(rows * u + lo, 16), 64)
+            for lo in range(0, rows, 64):
+                where = slice(rows * u + lo, rows * u + lo + 64)
                 buffers[i][where, :] = (g[i][where, :].astype(F32) * factor).astype(BF)
 
-            for_rows(rows, 64, body)
             if kind == 2:
                 half = pl.ds(2 * DN * j, 2 * DN)
                 start(buffers[i].at[at, pl.ds(0, 2 * DN)], k_out.at[at, half])
@@ -505,7 +506,7 @@
         in_specs=[vmem] * (G + 2),
         out_specs=(hbm,) * 5,
         scratch_shapes=[pltpu.VMEM(SHAPES[i % 3], BF) for i in range(G)]
-        + [pltpu.VMEM((8, KL + DR), F32), pltpu.SemaphoreType.DMA((2 + SUB * PAIRS * 4,))],
+        + [pltpu.VMEM((8, KL + DR), F32), pltpu.SemaphoreType.DMA((2 + CUTS * PAIRS * 4,))],
         name="finish",
         compiler_params=pltpu.CompilerParams(vmem_limit_bytes=16 << 20),
     )(s, lat, *pieces)

time: 61.4 us -> 61.4 us (level)
  no operation moved by 1% of the time
where the time goes in v5:
time: 61.4 us; the launch traced here: 61.3 us
  Pallas kernels  60.7 us (99%)
  between operations  0.64 us (1%)
    pallas_call x1, Pallas kernels, step(): pl.pallas_call(step_kernel, out_shape=tuple((jax.ShapeDtypeStruct(SHAPES[...  58.6 us
    pallas_call x1, Pallas kernels, finish(): pl.pallas_call(functools.partial(finish_kernel, count), out_shape=(jax.Sh...  2.05 us

profile of v5, /device:TPU:2, one launch (start us, length us, event | category | flops | bytes accessed | tf_op | source)
XLA Modules:
  0.0 61.3 jit_solution(11299479432330275879)
XLA Ops:
  0.6 58.6 %step.1 = (bf16[768,384]{1,0:T(8,128)(2,1)S(1)}, bf16[768,384]{1,0:T(8,128)(2,1)S(1)}, bf16[512,512]{1,0:T(8,128)(2,1)S(1)}, bf16[768,384]{1,0:T(8,128)(2,1)S(1)...) custom-call(bf16[256,1536]{1,0:T(8,128)(2,1)} %refs_0_.1, ...), custom_call_target="tpu_custom_call" | custom-call | tf_op jit(solution)/shard_map/step/pallas_call | solution.py:437
  59.3 2.0 %finish.1 = (f32[8,1536]{1,0:T(8,128)}, f32[8,576]{1,0:T(8,128)}, bf16[1536,768]{1,0:T(8,128)(2,1)}, bf16[512,512]{1,0:T(8,128)(2,1)}, bf16[512,512]{1,0:T(8,128)(2,1)}) custom-call(f32[8,8,128]{2,1,0:T(8,128)S(1)} %get-tuple-element.13.refs_0_, f32[8,2176]{1,0:T(8,128)S(1)} %get-tuple-element.14.refs_1_, bf16[768,384]{1,0:T(8,128)(2,1)S(1)} %get-tuple-element.15.refs_2_, ...), custom_call_target="tpu_custom_call" | custom-call | tf_op jit(solution)/shard_map/finish/pallas_call | solution.py:497
